TPU v7x, 32 devices: a whole 2x2x4 slice. The times are simulated.
32 devices in a mesh: row: 4 (over z), col: 4 (over y, core), ch: 2 (over x).
Axes of the slice: x: 2, y: 2, z: 4, core: 2. Of those that a mesh axis runs over, the one named last changes fastest.
Arguments:
- spectra: float32 [384, 128, 1024], P('ch', 'row', 'col'), may hold values from 0 to 1
- pixel_factor: float32 [64, 128, 1024], P(None, 'row', 'col'), may hold values from 0.1 to 1
- channel_factor: float32 [64, 384], P(None, 'ch'), may hold values from 0.1 to 1
- labels: int32 [128, 1024], P('row', 'col'), may hold values from 0 to 3
Outputs:
- smoothed_factor: float32 [64, 128, 1024], P(None, 'row', 'col')
- new_channel: float32 [64, 384], P(None, 'ch')
All inputs are finite; a program needn't handle non-finite values.
Results may differ from a plain program's by a relative error of at most 0.000068.
Values sent between devices are 32-bit elements; how exact they have to be, the bound alone decides.
A program may use at most 64 MiB of HBM per device.

v0:
```python
import functools

import jax
import jax.numpy as jnp
from jax import lax
from jax.experimental import pallas as pl
from jax.experimental.pallas import tpu as pltpu
from jax.sharding import PartitionSpec as P

SMOOTH = 3
MESH = pl.DeviceIdType.MESH
LANES = 128
SUB = 8
CHUNK = 2
EDGE = -(-SMOOTH // CHUNK)
LAG = 4

epsilon = 1e-09


def split(value):
    high = value.astype(jnp.bfloat16)
    low = (value - high.astype(jnp.float32)).astype(jnp.bfloat16)
    return high, low


def dot(left, right, contraction):
    return lax.dot_general(
        left, right, (contraction, ((), ())), preferred_element_type=jnp.float32
    )


def dot3(left, right, contraction):
    rows = left[0].shape[0]
    both = dot(jnp.concatenate(left, axis=0), right[0], contraction)
    return both[:rows] + both[rows:] + dot(left[0], right[1], contraction)


NT = ((1,), (1,))
NN = ((1,), (0,))


def factor_kernel(
    sizes, x_hbm, w_hbm, cf_ref, lab_ref, out_hbm, nc_out,
    xs, ws, other, gram, gram_in, gram_row, nc, part, field, left, right, weight, first, second, done,
    load_sem, e_send, e_recv, g_send, g_recv, z_send, z_recv, n_send, n_recv,
    t_send, t_recv, c_send, c_recv, r_send, r_recv, out_sem,
):
    n_row, n_col, n_ch = sizes
    rank, rows, cols = w_hbm.shape
    chans = x_hbm.shape[0]
    share = rank // n_col
    chunks = rows // CHUNK
    early = rows - EDGE * CHUNK
    wide = cols + LANES
    me_row, me_col, me_ch = (lax.axis_index(a) for a in ("row", "col", "ch"))

    halves = cols // LANES
    groups = rows // SUB

    def load(g):
        for h in range(halves):
            for j, (source, target) in enumerate(((w_hbm, ws), (x_hbm, xs))):
                at = (slice(None), pl.ds(g * SUB, SUB))
                yield pltpu.make_async_copy(
                    source.at[at + (pl.ds(h * LANES, LANES),)],
                    target.at[(h,) + at + (slice(None),)],
                    load_sem.at[j, h, g],
                )

    def image_row(buffer, r):
        _, depth, tall, _ = buffer.shape
        return jnp.concatenate(
            [
                buffer.at[h].reshape(depth * tall, LANES)[pl.ds(r, depth, stride=tall), :]
                for h in range(halves)
            ],
            axis=1,
        )

    order = tuple(range(groups - 1, -1, -1))
    for g in order:
        for copy in load(g):
            copy.start()

    barrier = pltpu.get_barrier_semaphore()
    for d in range(1, n_row):
        pl.semaphore_signal(
            barrier, inc=1, device_id={"row": lax.rem(me_row + d, n_row)}, device_id_type=MESH
        )
    for d in range(1, n_col * n_ch):
        pl.semaphore_signal(
            barrier, inc=1, device_id=side(me_col, me_ch, d, n_col, n_ch), device_id_type=MESH
        )

    for buffer in (left, right):
        edge = 0 if buffer is left else n_col - 1

        @pl.when(me_col == edge)
        def _():
            buffer[...] = jnp.zeros_like(buffer)

    for at, edge in ((0, 0), (rows + SMOOTH, n_row - 1)):

        @pl.when(me_row == edge)
        def _():
            field[pl.ds(at, SMOOTH)] = jnp.zeros((SMOOTH,) + field.shape[1:], jnp.float32)

    def marks(r, carry):
        row = (lab_ref[pl.ds(r, 1), :] + 1).astype(jnp.float32)
        field[r + SMOOTH, pl.ds(rank, SUB), pl.ds(0, cols)] = jnp.broadcast_to(row, (SUB, cols))
        return carry

    lax.fori_loop(0, rows, marks, 0)

    gram[...] = jnp.zeros_like(gram)

    def to_early(d):
        return pltpu.make_async_remote_copy(
            xs.at[:, :, pl.ds(early, rows - early), :],
            other.at[d - 1, :, :, pl.ds(early - rows + SUB, rows - early), :],
            e_send.at[d - 1], e_recv.at[d - 1],
            device_id={"ch": lax.rem(me_ch + d, n_ch)}, device_id_type=MESH,
        )

    for i, g in enumerate(order):
        for copy in load(g):
            copy.wait()
        if i == 0:
            pl.semaphore_wait(barrier, n_row - 1 + n_col * n_ch - 1)
            for d in range(1, n_ch):
                to_early(d).start()
        for r in range(g * SUB, g * SUB + SUB):
            both = jnp.concatenate([image_row(ws, r), image_row(xs, r)], axis=0)
            high, low = split(both)
            total = dot3((high[:rank], low[:rank]), (high, low), NT)
            gram[...] += total.reshape(gram.shape)

    def to_col(d):
        peer = lax.rem(me_col + d, n_col)
        return pltpu.make_async_remote_copy(
            gram.at[peer], gram_in.at[d - 1], g_send.at[d - 1], g_recv.at[d - 1],
            device_id={"col": peer}, device_id_type=MESH,
        )

    for d in range(1, n_col):
        to_col(d).start()
    own = gram[me_col]
    for d in range(1, n_col):
        to_col(d).wait_recv()
        own = own + gram_in[d - 1]
    gram_row[me_row] = own

    def to_row(d):
        peer = lax.rem(me_row + d, n_row)
        return pltpu.make_async_remote_copy(
            gram_row.at[me_row], gram_row.at[me_row], z_send.at[d - 1], z_recv.at[d - 1],
            device_id={"row": peer}, device_id_type=MESH,
        )

    def from_row(d):
        peer = lax.rem(me_row + n_row - d, n_row)
        return pltpu.make_async_remote_copy(
            gram_row.at[peer], gram_row.at[peer], z_send.at[d - 1], z_recv.at[d - 1],
            device_id={"row": peer}, device_id_type=MESH,
        )

    for d in range(1, n_row):
        to_row(d).start()
    for d in range(1, n_row):
        from_row(d).wait_recv()
    total = gram_row[0]
    for z in range(1, n_row):
        total = total + gram_row[z]
    lower = jnp.dot(
        total[:, :rank], cf_ref[...], precision=lax.Precision.HIGHEST,
        preferred_element_type=jnp.float32,
    )
    own_cf = cf_ref[pl.ds(pl.multiple_of(me_col * share, share), share), :]
    nc[me_ch, me_col] = own_cf * total[:, rank:] / (lower + epsilon)

    def to_side(d):
        return pltpu.make_async_remote_copy(
            nc.at[me_ch, me_col], nc.at[me_ch, me_col], n_send.at[d - 1], n_recv.at[d - 1],
            device_id=side(me_col, me_ch, d, n_col, n_ch), device_id_type=MESH,
        )

    def from_side(d):
        at = side(me_col, me_ch, n_col * n_ch - d, n_col, n_ch)
        slot = nc.at[at["ch"], at["col"]]
        return pltpu.make_async_remote_copy(
            slot, slot, n_send.at[d - 1], n_recv.at[d - 1],
            device_id=at, device_id_type=MESH,
        )

    for d in range(1, n_col * n_ch):
        to_side(d).start()
    for d in range(1, n_col * n_ch):
        from_side(d).wait_recv()

    mine = nc[me_ch].reshape(rank, chans)
    nc_out[...] = mine
    mine = split(mine)

    def chunk_of(i):
        return lax.rem(i + chunks - EDGE, chunks)

    def to_ch(d, c):
        peer = lax.rem(me_ch + d, n_ch)
        slot = part.at[me_ch, pl.ds(c * CHUNK, CHUNK)]
        return pltpu.make_async_remote_copy(
            slot, slot, t_send.at[d - 1, c], t_recv.at[d - 1, c],
            device_id={"ch": peer}, device_id_type=MESH,
        )

    def from_ch(d, c):
        peer = lax.rem(me_ch + n_ch - d, n_ch)
        slot = part.at[peer, pl.ds(c * CHUNK, CHUNK)]
        return pltpu.make_async_remote_copy(
            slot, slot, t_send.at[d - 1, c], t_recv.at[d - 1, c],
            device_id={"ch": peer}, device_id_type=MESH,
        )

    def send_part(i, carry):
        c = chunk_of(i)
        for k in range(CHUNK):
            r = c * CHUNK + k
            part[me_ch, r] = dot3(mine, split(image_row(xs, r)), NN)
        for d in range(1, n_ch):
            to_ch(d, c).start()
        return carry

    lax.fori_loop(EDGE, chunks, send_part, 0)

    for r in range(early, rows):
        part[me_ch, r] = dot3(mine, split(image_row(xs, r)), NN)
    for d in range(1, n_ch):
        peer = lax.rem(me_ch + n_ch - d, n_ch)
        theirs = split(nc[peer].reshape(rank, chans))
        to_early(d).wait_recv()
        for r in range(early, rows):
            part[peer, r] = dot3(theirs, split(image_row(other.at[d - 1], r - rows + SUB)), NN)

    cg = jnp.zeros((rank, rank), jnp.float32)
    for h in range(n_ch):
        block = nc[h].reshape(rank, chans)
        cg = cg + lax.dot_general(
            block, block, (NT, ((), ())), precision=lax.Precision.HIGHEST,
            preferred_element_type=jnp.float32,
        )
    cg = split(cg)

    def to_right(c):
        return pltpu.make_async_remote_copy(
            field.at[pl.ds(c * CHUNK + SMOOTH, CHUNK), :, pl.ds(cols - LANES, LANES)],
            left.at[pl.ds(c * CHUNK, CHUNK)], c_send.at[0, c], c_recv.at[0, c],
            device_id={"col": lax.rem(me_col + 1, n_col)}, device_id_type=MESH,
        )

    def to_left(c):
        return pltpu.make_async_remote_copy(
            field.at[pl.ds(c * CHUNK + SMOOTH, CHUNK), :, pl.ds(0, LANES)],
            right.at[pl.ds(c * CHUNK, CHUNK)], c_send.at[1, c], c_recv.at[1, c],
            device_id={"col": lax.rem(me_col + n_col - 1, n_col)}, device_id_type=MESH,
        )

    def raise_chunk(i, awaited=True):
        c = chunk_of(i)
        if awaited:
            for d in range(1, n_ch):
                from_ch(d, c).wait_recv()
        for k in range(CHUNK):
            r = c * CHUNK + k
            w = image_row(ws, r)
            top = part[0, r]
            for h in range(1, n_ch):
                top = top + part[h, r]
            low = dot3(cg, split(w), NN)
            field[r + SMOOTH, pl.ds(0, rank), pl.ds(0, cols)] = w * top / (low + epsilon)

        @pl.when(me_col < n_col - 1)
        def _():
            to_right(c).start()

        @pl.when(me_col > 0)
        def _():
            to_left(c).start()

    lane = lax.broadcasted_iota(jnp.int32, (CHUNK, rank + SUB, LANES), 2)

    def widen_chunk(i):
        c = chunk_of(i)

        @pl.when(me_col > 0)
        def _():
            to_right(c).wait_recv()

        @pl.when(me_col < n_col - 1)
        def _():
            to_left(c).wait_recv()

        from_right = jnp.where(lane < SMOOTH, right[pl.ds(c * CHUNK, CHUNK)], 0.0)
        wide = jnp.where(lane >= LANES - SMOOTH, left[pl.ds(c * CHUNK, CHUNK)], from_right)
        field[pl.ds(c * CHUNK + SMOOTH, CHUNK), :, pl.ds(cols, LANES)] = wide

    def to_down():
        return pltpu.make_async_remote_copy(
            field.at[pl.ds(rows, SMOOTH)], field.at[pl.ds(0, SMOOTH)], r_send.at[0], r_recv.at[0],
            device_id={"row": lax.rem(me_row + 1, n_row)}, device_id_type=MESH,
        )

    def to_up():
        return pltpu.make_async_remote_copy(
            field.at[pl.ds(SMOOTH, SMOOTH)], field.at[pl.ds(rows + SMOOTH, SMOOTH)],
            r_send.at[1], r_recv.at[1],
            device_id={"row": lax.rem(me_row + n_row - 1, n_row)}, device_id_type=MESH,
        )

    def coefficients(e):
        center = field[e, pl.ds(rank, SUB), :]
        around = (
            field[e - 1, pl.ds(rank, SUB), :],
            field[e + 1, pl.ds(rank, SUB), :],
            pltpu.roll(center, 1, 1),
            pltpu.roll(center, wide - 1, 1),
        )
        parts = [
            jnp.where(near == 0, 0.0, jnp.where(near == center, 1.0, 0.25)) for near in around
        ]
        scale = 1.0 / (1.0 + parts[0] + parts[1] + parts[2] + parts[3])
        weight[e, 0] = scale
        for j in range(4):
            weight[e, j + 1] = parts[j] * scale

    def smooth(source, e):
        here, up, down = (
            source[at, pl.ds(0, rank), :].reshape(rank // SUB, SUB, wide)
            for at in (e, e - 1, e + 1)
        )
        total = weight[e, 0] * here + weight[e, 1] * up + weight[e, 2] * down
        total = total + weight[e, 3] * pltpu.roll(here, 1, 2)
        total = total + weight[e, 4] * pltpu.roll(here, wide - 1, 2)
        return total.reshape(rank, wide)

    def put(r):
        return pltpu.make_async_copy(done.at[r], out_hbm.at[:, r, :], out_sem.at[r])

    def one(e, carry):
        coefficients(e)
        first[e] = smooth(field, e)
        return carry

    def two(e, carry):
        second[e] = smooth(first, e)
        return carry

    def three(e, carry):
        done[e - SMOOTH] = smooth(second, e)[:, :cols]
        put(e - SMOOTH).start()
        return carry

    def sweep(starts, counts):
        for stage, start, count in zip((one, two, three), starts, counts):
            lax.fori_loop(0, count, lambda k, v, f=stage, s=start: f(s + k, v), 0)

    def sweep_chunk(c):
        sweep((CHUNK * c + 2, CHUNK * c + 1, CHUNK * c), (CHUNK,) * 3)

    for i in range(2 * EDGE):
        raise_chunk(i, awaited=i >= EDGE)
    for i in range(2 * EDGE):
        widen_chunk(i)

    @pl.when(me_row < n_row - 1)
    def _():
        to_down().start()

    @pl.when(me_row > 0)
    def _():
        to_up().start()

    for i in range(2 * EDGE, 2 * EDGE + LAG):
        raise_chunk(i)
        if i > 2 * EDGE + 1:
            widen_chunk(i - 2)

    @pl.when(me_row > 0)
    def _():
        to_down().wait_recv()

    @pl.when(me_row < n_row - 1)
    def _():
        to_up().wait_recv()

    tip = CHUNK * EDGE
    sweep((1, 2, 3), (tip + 1, tip - 1, tip - 3))
    for c in range(EDGE, EDGE + LAG - 2):
        sweep_chunk(c)

    def step(i, carry):
        widen_chunk(i - 2)
        sweep_chunk(i - 2 - EDGE)
        raise_chunk(i)
        return carry

    lax.fori_loop(2 * EDGE + LAG, chunks, step, 0)
    for i in (chunks - 2, chunks - 1):
        widen_chunk(i)
        sweep_chunk(i - EDGE)
    sweep((early + 2, early + 1, early), (tip + 3,) * 3)

    for d in range(1, n_col):
        to_col(d).wait_send()
    for d in range(1, n_row):
        to_row(d).wait_send()
    for d in range(1, n_col * n_ch):
        to_side(d).wait_send()

    def drain(c, carry):
        @pl.when(me_col < n_col - 1)
        def _():
            to_right(c).wait_send()

        @pl.when(me_col > 0)
        def _():
            to_left(c).wait_send()

        return carry

    lax.fori_loop(0, chunks, drain, 0)

    def drain_part(i, carry):
        for d in range(1, n_ch):
            to_ch(d, chunk_of(i)).wait_send()
        return carry

    lax.fori_loop(EDGE, chunks, drain_part, 0)
    for d in range(1, n_ch):
        to_early(d).wait_send()

    @pl.when(me_row < n_row - 1)
    def _():
        to_down().wait_send()

    @pl.when(me_row > 0)
    def _():
        to_up().wait_send()

    def drain_out(r, carry):
        put(r).wait()
        return carry

    lax.fori_loop(0, rows, drain_out, 0)


def side(me_col, me_ch, d, n_col, n_ch):
    place = lax.rem(me_col * n_ch + me_ch + d, n_col * n_ch)
    return {"col": place // n_ch, "ch": lax.rem(place, n_ch)}


def shards(sizes, spectra, pixel_factor, channel_factor, labels):
    n_row, n_col, n_ch = sizes
    rank, rows, cols = pixel_factor.shape
    chans = spectra.shape[0]
    share = rank // n_col
    chunks = rows // CHUNK
    tall = rows + 2 * SMOOTH
    wide = cols + LANES
    f32 = jnp.float32
    vmem = pl.BlockSpec(memory_space=pltpu.VMEM)
    anywhere = pl.BlockSpec(memory_space=pl.ANY)
    dma = pltpu.SemaphoreType.DMA
    return pl.pallas_call(
        functools.partial(factor_kernel, sizes),
        out_shape=(
            jax.ShapeDtypeStruct(pixel_factor.shape, f32),
            jax.ShapeDtypeStruct(channel_factor.shape, f32),
        ),
        in_specs=[anywhere, anywhere, vmem, vmem],
        out_specs=(anywhere, vmem),
        scratch_shapes=[
            pltpu.VMEM((cols // LANES, chans, rows, LANES), f32),
            pltpu.VMEM((cols // LANES, rank, rows, LANES), f32),
            pltpu.VMEM((n_ch - 1, cols // LANES, chans, SUB, LANES), f32),
            pltpu.VMEM((n_col, share, rank + chans), f32),
            pltpu.VMEM((n_col - 1, share, rank + chans), f32),
            pltpu.VMEM((n_row, share, rank + chans), f32),
            pltpu.VMEM((n_ch, n_col, share, chans), f32),
            pltpu.VMEM((n_ch, rows, rank, cols), f32),
            pltpu.VMEM((tall, rank + SUB, wide), f32),
            pltpu.VMEM((rows, rank + SUB, LANES), f32),
            pltpu.VMEM((rows, rank + SUB, LANES), f32),
            pltpu.VMEM((tall, 5, SUB, wide), f32),
            pltpu.VMEM((tall, rank, wide), f32),
            pltpu.VMEM((tall, rank, wide), f32),
            pltpu.VMEM((rows, rank, cols), f32),
            dma((2, cols // LANES, rows // SUB)),
            dma((n_ch - 1,)), dma((n_ch - 1,)),
            dma((n_col - 1,)), dma((n_col - 1,)),
            dma((n_row - 1,)), dma((n_row - 1,)),
            dma((n_col * n_ch - 1,)), dma((n_col * n_ch - 1,)),
            dma((n_ch - 1, chunks)), dma((n_ch - 1, chunks)),
            dma((2, chunks)), dma((2, chunks)),
            dma((2,)), dma((2,)),
            dma((rows,)),
        ],
        compiler_params=pltpu.CompilerParams(
            collective_id=0, has_side_effects=True, vmem_limit_bytes=60 * 1024 * 1024
        ),
        name="factor",
    )(spectra, pixel_factor, channel_factor, labels)


def solution(mesh):
    sizes = tuple(mesh.shape[a] for a in ("row", "col", "ch"))
    placed = (P("ch", "row", "col"), P(None, "row", "col"), P(None, "ch"), P("row", "col"))
    return jax.shard_map(
        functools.partial(shards, sizes),
        mesh=mesh,
        in_specs=placed,
        out_specs=(P(None, "row", "col"), P(None, "ch")),
        check_vma=False,
    )
```

profile of v0, /device:TPU:1, one launch (start us, length us, event | category | flops | bytes accessed | tf_op | source)
XLA Modules:
  0.0 81.7 jit_solution(16996479479510228968)
XLA Ops:
  0.6 77.2 %factor.1 = (f32[64,32,256]{2,1,0:T(8,128)}, f32[64,192]{1,0:T(8,128)}) custom-call(f32[192,32,256]{2,1,0:T(8,128)} %x_hbm.1, f32[64,32,256]{2,1,0:T(8,128)} %w_hbm.1, f32[64,192]{1,0:T(8,128)} %cf_ref.1, s32[32,256]{1,0:T(8,128)} %lab_ref.1), custom_call_target="tpu_custom_call" | custom-call | tf_op jit(solution)/shard_map/factor/pallas_call | solution.py:473
  77.8 0.0 copy-start
  77.8 3.2 %copy.8 = f32[64,32,256]{2,1,0:T(8,128)} copy(f32[64,32,256]{2,1,0:T(8,128)} %get-tuple-element.4) | data formatting | bytes 4194304
  81.0 0.0 copy-done
  81.0 0.6 copy.9
Async XLA Ops:
  77.8 3.2 %copy-start = (f32[64,192]{1,0:T(8,128)S(1)}, f32[64,192]{1,0:T(8,128)}, u32[]{:S(2)}) copy-start(f32[64,192]{1,0:T(8,128)} %get-tuple-element.5) | copy-start | bytes 147460
where the time goes:
time: 81.9 us; the launch traced here: 81.7 us
  Pallas kernels  77.2 us (94%)
  local copies, waits for them, and re-layouts  3.82 us (5%)
    pallas_call x1, Pallas kernels, shards(): pl.pallas_call(functools.partial(factor_kernel, sizes), out_shape=(jax.Sh...  77.2 us
    unnamed x4, local copies, waits for them, and re-layouts  3.82 us

commit v1 on v0

v1 whole, which is shorter than its diff:
```python
import functools

import jax
import jax.numpy as jnp
from jax import lax
from jax.experimental import pallas as pl
from jax.experimental.pallas import tpu as pltpu
from jax.sharding import PartitionSpec as P

SMOOTH = 3
MESH = pl.DeviceIdType.MESH
LANES = 128
SUB = 8
CHUNK = 2
EARLY = 3
BAND = 8

epsilon = 1e-09


def split(value):
    high = value.astype(jnp.bfloat16)
    low = (value - high.astype(jnp.float32)).astype(jnp.bfloat16)
    return high, low


def dot(left, right, contraction):
    return lax.dot_general(
        left, right, (contraction, ((), ())), preferred_element_type=jnp.float32
    )


def dot3(left, right, contraction):
    rows = left[0].shape[0]
    both = dot(jnp.concatenate(left, axis=0), right[0], contraction)
    return both[:rows] + both[rows:] + dot(left[0], right[1], contraction)


NT = ((1,), (1,))
NN = ((1,), (0,))


def factor_kernel(
    sizes, x_hbm, w_hbm, cf_ref, lab_ref, out_hbm, nc_out,
    xs, ws, high, low, other, gram, gram_in, gram_row, nc, part, scale, field, left, right,
    mark, mark_left, mark_right, weight, first, second, done,
    load_sem, e_send, e_recv, g_send, g_recv, z_send, z_recv, n_send, n_recv,
    t_send, t_recv, c_send, c_recv, r_send, r_recv, m_send, m_recv, out_sem,
):
    n_row, n_col, n_ch = sizes
    rank, rows, cols = w_hbm.shape
    chans = x_hbm.shape[0]
    share = rank // n_col
    early = rows - EARLY
    chunks = (early - SMOOTH) // CHUNK
    main = chunks * CHUNK
    tip = early - main
    bands = rank // BAND
    tall = rows + 2 * SMOOTH
    wide = cols + LANES
    me_row, me_col, me_ch = (lax.axis_index(a) for a in ("row", "col", "ch"))

    halves = cols // LANES
    groups = rows // SUB

    def load(g):
        start = pl.multiple_of(g * SUB, SUB)
        for h in range(halves):
            for j, (source, target) in enumerate(((w_hbm, ws), (x_hbm, xs))):
                yield pltpu.make_async_copy(
                    source.at[:, pl.ds(start, SUB), pl.ds(h * LANES, LANES)],
                    target.at[g, h],
                    load_sem.at[j, h, g],
                )

    def image_row(buffer, s):
        _, depth, _, _ = buffer.shape
        return jnp.concatenate(
            [
                buffer.at[h].reshape(depth * SUB, LANES)[pl.ds(s, depth, stride=SUB), :]
                for h in range(halves)
            ],
            axis=1,
        )

    for g in range(groups):
        for copy in load(g):
            copy.start()

    barrier = pltpu.get_barrier_semaphore()
    for d in range(1, n_row):
        pl.semaphore_signal(
            barrier, inc=1, device_id={"row": lax.rem(me_row + d, n_row)}, device_id_type=MESH
        )
    for d in range(1, n_col * n_ch):
        pl.semaphore_signal(
            barrier, inc=1, device_id=side(me_col, me_ch, d, n_col, n_ch), device_id_type=MESH
        )

    for buffer, edge in (
        (left, 0), (mark_left, 0), (right, n_col - 1), (mark_right, n_col - 1),
    ):

        @pl.when(me_col == edge)
        def _():
            buffer[...] = jnp.zeros_like(buffer)

    for at, edge in ((0, 0), (rows + SMOOTH, n_row - 1)):
        for buffer in (field, mark):

            @pl.when(me_row == edge)
            def _():
                buffer[pl.ds(at, SMOOTH)] = jnp.zeros((SMOOTH,) + buffer.shape[1:], jnp.float32)

    def marks(r, carry):
        row = (lab_ref[pl.ds(r, 1), :] + 1).astype(jnp.float32)
        mark[r + SMOOTH, :, pl.ds(0, cols)] = jnp.broadcast_to(row, (SUB, cols))
        return carry

    lax.fori_loop(0, rows, marks, 0)

    gram[...] = jnp.zeros_like(gram)

    def to_early(d, h):
        return pltpu.make_async_remote_copy(
            x_hbm.at[:, pl.ds(early, EARLY), pl.ds(h * LANES, LANES)],
            other.at[d - 1, h, :, pl.ds(SUB - EARLY, EARLY), :],
            e_send.at[d - 1, h], e_recv.at[d - 1, h],
            device_id={"ch": lax.rem(me_ch + d, n_ch)}, device_id_type=MESH,
        )

    def beside(step, source, target, at):
        return pltpu.make_async_remote_copy(
            source, target, *at, device_id={"col": lax.rem(me_col + n_col + step, n_col)},
            device_id_type=MESH,
        )

    def mark_side(step):
        k, start, target = ((0, cols - LANES, mark_left), (1, 0, mark_right))[step < 0]
        return beside(
            step, mark.at[pl.ds(SMOOTH, rows), :, pl.ds(start, LANES)], target,
            (m_send.at[k], m_recv.at[k]),
        )

    def across(step, buffer, at):
        start, end = ((rows, 0), (SMOOTH, rows + SMOOTH))[step < 0]
        return pltpu.make_async_remote_copy(
            buffer.at[pl.ds(start, SMOOTH)], buffer.at[pl.ds(end, SMOOTH)], *at,
            device_id={"row": lax.rem(me_row + n_row + step, n_row)}, device_id_type=MESH,
        )

    def mark_across(step):
        k = 2 + (step < 0)
        return across(step, mark, (m_send.at[k], m_recv.at[k]))

    def field_across(step):
        k = int(step < 0)
        return across(step, field, (r_send.at[k], r_recv.at[k]))

    def start_pair(copy, me, n):
        @pl.when(me < n - 1)
        def _():
            copy(1).start()

        @pl.when(me > 0)
        def _():
            copy(-1).start()

    def receive_pair(copy, me, n):
        @pl.when(me > 0)
        def _():
            copy(1).wait_recv()

        @pl.when(me < n - 1)
        def _():
            copy(-1).wait_recv()

    def sent_pair(copy, me, n):
        @pl.when(me < n - 1)
        def _():
            copy(1).wait_send()

        @pl.when(me > 0)
        def _():
            copy(-1).wait_send()

    pl.semaphore_wait(barrier, n_row - 1 + n_col * n_ch - 1)
    for d in range(1, n_ch):
        for h in range(halves):
            to_early(d, h).start()
    start_pair(mark_side, me_col, n_col)

    def gather(g, carry):
        for copy in load(g):
            copy.wait()
        upper = lower = 0.0
        for s in range(SUB):
            both = jnp.concatenate([image_row(ws.at[g], s), image_row(xs.at[g], s)], axis=0)
            h, l = split(both)
            high[g * SUB + s] = h
            low[g * SUB + s] = l
            upper = upper + dot(jnp.concatenate([h[:rank], l[:rank]], axis=0), h, NT)
            lower = lower + dot(h[:rank], l, NT)
        gram[...] += (upper[:rank] + upper[rank:] + lower).reshape(gram.shape)
        return carry

    lax.fori_loop(0, groups, gather, 0)

    def to_col(d):
        peer = lax.rem(me_col + d, n_col)
        return pltpu.make_async_remote_copy(
            gram.at[peer], gram_in.at[d - 1], g_send.at[d - 1], g_recv.at[d - 1],
            device_id={"col": peer}, device_id_type=MESH,
        )

    for d in range(1, n_col):
        to_col(d).start()

    lane = lax.broadcasted_iota(jnp.int32, (1, SUB, LANES), 2)

    def joined(from_left, from_right):
        return jnp.where(
            lane >= LANES - SMOOTH, from_left, jnp.where(lane < SMOOTH, from_right, 0.0)
        )

    receive_pair(mark_side, me_col, n_col)
    mark[pl.ds(SMOOTH, rows), :, pl.ds(cols, LANES)] = joined(mark_left[...], mark_right[...])
    start_pair(mark_across, me_row, n_row)

    own = gram[me_col]
    for d in range(1, n_col):
        to_col(d).wait_recv()
        own = own + gram_in[d - 1]
    gram_row[me_row] = own

    def to_row(d):
        peer = lax.rem(me_row + d, n_row)
        return pltpu.make_async_remote_copy(
            gram_row.at[me_row], gram_row.at[me_row], z_send.at[d - 1], z_recv.at[d - 1],
            device_id={"row": peer}, device_id_type=MESH,
        )

    def from_row(d):
        peer = lax.rem(me_row + n_row - d, n_row)
        return pltpu.make_async_remote_copy(
            gram_row.at[peer], gram_row.at[peer], z_send.at[d - 1], z_recv.at[d - 1],
            device_id={"row": peer}, device_id_type=MESH,
        )

    for d in range(1, n_row):
        to_row(d).start()

    receive_pair(mark_across, me_row, n_row)

    def coefficients(e, carry):
        center = mark[e]
        around = (
            mark[e - 1], mark[e + 1], pltpu.roll(center, 1, 1), pltpu.roll(center, wide - 1, 1)
        )
        parts = [
            jnp.where(near == 0, 0.0, jnp.where(near == center, 1.0, 0.25)) for near in around
        ]
        own_scale = 1.0 / (1.0 + parts[0] + parts[1] + parts[2] + parts[3])
        weight[e, 0] = own_scale
        for j in range(4):
            weight[e, j + 1] = parts[j] * own_scale
        return carry

    lax.fori_loop(1, tall - 1, coefficients, 0)

    for d in range(1, n_row):
        from_row(d).wait_recv()
    total = gram_row[0]
    for z in range(1, n_row):
        total = total + gram_row[z]
    under = jnp.dot(
        total[:, :rank], cf_ref[...], precision=lax.Precision.HIGHEST,
        preferred_element_type=jnp.float32,
    )
    own_cf = cf_ref[pl.ds(pl.multiple_of(me_col * share, share), share), :]
    nc[me_ch, me_col] = own_cf * total[:, rank:] / (under + epsilon)

    def to_side(d):
        return pltpu.make_async_remote_copy(
            nc.at[me_ch, me_col], nc.at[me_ch, me_col], n_send.at[d - 1], n_recv.at[d - 1],
            device_id=side(me_col, me_ch, d, n_col, n_ch), device_id_type=MESH,
        )

    def from_side(d):
        at = side(me_col, me_ch, n_col * n_ch - d, n_col, n_ch)
        slot = nc.at[at["ch"], at["col"]]
        return pltpu.make_async_remote_copy(
            slot, slot, n_send.at[d - 1], n_recv.at[d - 1],
            device_id=at, device_id_type=MESH,
        )

    same = [d for d in range(1, n_col * n_ch) if d % n_ch == 0]
    away = [d for d in range(1, n_col * n_ch) if d % n_ch]
    for d in same + away:
        to_side(d).start()
    for d in same:
        from_side(d).wait_recv()

    mine = nc[me_ch].reshape(rank, chans)
    nc_out[...] = mine

    def stacked(value):
        h, l = split(value)
        return jnp.concatenate([h, l], axis=0)

    mine = stacked(mine)

    def product(pair, h, l):
        depth = pair.shape[0] // 2
        both = dot(pair, h, NN)
        return both[:depth] + both[depth:] + dot(pair[:depth], l, NN)

    def own_part(r):
        at = (pl.ds(rank, chans), slice(None))
        part[me_ch, r] = product(mine, high[(r,) + at], low[(r,) + at])

    def part_copy(d, peer, slot, k):
        return pltpu.make_async_remote_copy(
            slot, slot, t_send.at[d - 1, k], t_recv.at[d - 1, k],
            device_id={"ch": peer}, device_id_type=MESH,
        )

    def chunk_slot(h, c):
        return part.at[h, pl.ds(c * CHUNK, CHUNK)]

    def band_slot(h, q):
        return part.at[h, pl.ds(main, tip), pl.ds(pl.multiple_of(q * BAND, BAND), BAND)]

    def to_ch(d, slot, i, k):
        return part_copy(d, lax.rem(me_ch + d, n_ch), slot(me_ch, i), k)

    def from_ch(d, slot, i, k):
        peer = lax.rem(me_ch + n_ch - d, n_ch)
        return part_copy(d, peer, slot(peer, i), k)

    def send_part(c, carry):
        for k in range(CHUNK):
            own_part(c * CHUNK + k)
        for d in range(1, n_ch):
            to_ch(d, chunk_slot, c, c).start()
        return carry

    lax.fori_loop(0, chunks, send_part, 0)
    for r in range(main, early):
        own_part(r)
    for q in range(bands):
        for d in range(1, n_ch):
            to_ch(d, band_slot, q, chunks + q).start()

    for d in away:
        from_side(d).wait_recv()

    def channel_gram(h):
        block = nc[h].reshape(rank, chans)
        return lax.dot_general(
            block, block, (NT, ((), ())), precision=lax.Precision.HIGHEST,
            preferred_element_type=jnp.float32,
        )

    cg = channel_gram(0)
    for h in range(1, n_ch):
        cg = cg + channel_gram(h)
    cg = stacked(cg)

    def scales(r, carry):
        g, s = r // SUB, lax.rem(r, SUB)
        below = product(cg, high[r, pl.ds(0, rank), :], low[r, pl.ds(0, rank), :])
        scale[r] = image_row(ws.at[g], s) / (below + epsilon)
        return carry

    lax.fori_loop(0, rows, scales, 0)

    for r in range(early, rows):
        own_part(r)
    for d in range(1, n_ch):
        peer = lax.rem(me_ch + n_ch - d, n_ch)
        theirs = stacked(nc[peer].reshape(rank, chans))
        for h in range(halves):
            to_early(d, h).wait_recv()
        for r in range(early, rows):
            part[peer, r] = product(theirs, *split(image_row(other.at[d - 1], r - rows + SUB)))

    every = (0, rank)

    def field_side(start, count, band, k):
        def copy(step):
            j, lanes, target = ((0, cols - LANES, left), (1, 0, right))[step < 0]
            return beside(
                step,
                field.at[pl.ds(start + SMOOTH, count), pl.ds(*band), pl.ds(lanes, LANES)],
                target.at[pl.ds(start, count), pl.ds(*band)],
                (c_send.at[j, k], c_recv.at[j, k]),
            )
        return copy

    def raise_rows(start, count, band, k):
        at = (pl.ds(start, count), pl.ds(*band))
        top = part[(0,) + at]
        for h in range(1, n_ch):
            top = top + part[(h,) + at]
        field[pl.ds(start + SMOOTH, count), pl.ds(*band), pl.ds(0, cols)] = scale[at] * top
        start_pair(field_side(start, count, band, k), me_col, n_col)

    def widen_rows(start, count, band, k):
        receive_pair(field_side(start, count, band, k), me_col, n_col)
        at = (pl.ds(start, count), pl.ds(*band))
        shape = (count * band[1] // SUB, SUB, LANES)
        edge = joined(left[at].reshape(shape), right[at].reshape(shape))
        field[pl.ds(start + SMOOTH, count), pl.ds(*band), pl.ds(cols, LANES)] = edge.reshape(
            count, band[1], LANES
        )

    def raise_chunk(c):
        for d in range(1, n_ch):
            from_ch(d, chunk_slot, c, c).wait_recv()
        raise_rows(c * CHUNK, CHUNK, every, c)

    def widen_chunk(c):
        widen_rows(c * CHUNK, CHUNK, every, c)

    def smooth(source, e, band):
        here, up, down = (
            source[at, pl.ds(*band), :].reshape(band[1] // SUB, SUB, wide)
            for at in (e, e - 1, e + 1)
        )
        total = weight[e, 0] * here + weight[e, 1] * up + weight[e, 2] * down
        total = total + weight[e, 3] * pltpu.roll(here, 1, 2)
        total = total + weight[e, 4] * pltpu.roll(here, wide - 1, 2)
        return total.reshape(band[1], wide)

    def put(r):
        return pltpu.make_async_copy(done.at[r], out_hbm.at[:, r, :], out_sem.at[r])

    def one(e, band=every):
        first[e, pl.ds(*band), :] = smooth(field, e, band)

    def two(e, band=every):
        second[e, pl.ds(*band), :] = smooth(first, e, band)

    def three(e, band=every):
        done[e - SMOOTH, pl.ds(*band), :] = smooth(second, e, band)[:, :cols]

    def three_put(e):
        three(e)
        put(e - SMOOTH).start()

    def sweep(starts, counts):
        for stage, start, count in zip((one, two, three_put), starts, counts):
            def step(k, carry, f=stage, s=start):
                f(s + k)
                return carry
            lax.fori_loop(0, count, step, 0)

    def sweep_chunk(c):
        sweep((CHUNK * c + 2, CHUNK * c + 1, CHUNK * c), (CHUNK,) * 3)

    near = -(-SMOOTH // CHUNK)
    at_end = chunks + bands
    raise_rows(early, EARLY, every, at_end)
    for c in range(near):
        raise_chunk(c)
    widen_rows(early, EARLY, every, at_end)
    for c in range(near):
        widen_chunk(c)
    start_pair(field_across, me_row, n_row)
    for c in range(near, near + 2):
        raise_chunk(c)
    receive_pair(field_across, me_row, n_row)
    edge = early + SMOOTH
    last = rows + SMOOTH
    sweep((edge + 1, edge + 2, edge + 3), (last + 1 - edge, last - 1 - edge, max(last - 3 - edge, 0)))
    seen = near * CHUNK
    sweep((1, 2, 3), (seen + 1, seen - 1, seen - 3))

    def step(c, carry):
        widen_chunk(c - 2)
        sweep_chunk(c - 2)
        raise_chunk(c)
        return carry

    lax.fori_loop(near + 2, chunks, step, 0)

    def band_of(q):
        return (pl.multiple_of(q * BAND, BAND), BAND)

    def raise_band(q):
        for d in range(1, n_ch):
            from_ch(d, band_slot, q, chunks + q).wait_recv()
        raise_rows(main, tip, band_of(q), chunks + q)

    def finish_band(q):
        band = band_of(q)
        widen_rows(main, tip, band, chunks + q)
        for e in range(main + 2, edge + 1):
            one(e, band)
        for e in range(main + 1, edge + 2):
            two(e, band)
        for e in range(main, min(edge + 3, last)):
            three(e, band)

    widen_chunk(chunks - 2)
    sweep_chunk(chunks - 2)
    for q in range(2):
        raise_band(q)
    widen_chunk(chunks - 1)
    sweep_chunk(chunks - 1)

    def band_step(q, carry):
        finish_band(q - 2)
        raise_band(q)
        return carry

    lax.fori_loop(2, bands, band_step, 0)
    for q in (bands - 2, bands - 1):
        finish_band(q)
    for e in range(main, min(edge + 3, last)):
        put(e - SMOOTH).start()

    for d in range(1, n_col):
        to_col(d).wait_send()
    for d in range(1, n_row):
        to_row(d).wait_send()
    for d in range(1, n_col * n_ch):
        to_side(d).wait_send()
    sent_pair(mark_side, me_col, n_col)
    sent_pair(mark_across, me_row, n_row)
    sent_pair(field_across, me_row, n_row)
    sent_pair(field_side(early, EARLY, every, at_end), me_col, n_col)

    def drain_chunk(c, carry):
        sent_pair(field_side(c * CHUNK, CHUNK, every, c), me_col, n_col)
        for d in range(1, n_ch):
            to_ch(d, chunk_slot, c, c).wait_send()
        return carry

    lax.fori_loop(0, chunks, drain_chunk, 0)

    def drain_band(q, carry):
        sent_pair(field_side(main, tip, band_of(q), chunks + q), me_col, n_col)
        for d in range(1, n_ch):
            to_ch(d, band_slot, q, chunks + q).wait_send()
        return carry

    lax.fori_loop(0, bands, drain_band, 0)
    for d in range(1, n_ch):
        for h in range(halves):
            to_early(d, h).wait_send()

    def drain_out(r, carry):
        put(r).wait()
        return carry

    lax.fori_loop(0, rows, drain_out, 0)


def side(me_col, me_ch, d, n_col, n_ch):
    place = lax.rem(me_col * n_ch + me_ch + d, n_col * n_ch)
    return {"col": place // n_ch, "ch": lax.rem(place, n_ch)}


def shards(sizes, spectra, pixel_factor, channel_factor, labels):
    n_row, n_col, n_ch = sizes
    rank, rows, cols = pixel_factor.shape
    chans = spectra.shape[0]
    share = rank // n_col
    early = rows - EARLY
    pieces = (early - SMOOTH) // CHUNK + rank // BAND
    tall = rows + 2 * SMOOTH
    wide = cols + LANES
    halves, groups = cols // LANES, rows // SUB
    f32 = jnp.float32
    vmem = pl.BlockSpec(memory_space=pltpu.VMEM)
    anywhere = pl.BlockSpec(memory_space=pl.ANY)
    dma = pltpu.SemaphoreType.DMA
    return pl.pallas_call(
        functools.partial(factor_kernel, sizes),
        out_shape=(
            jax.ShapeDtypeStruct(pixel_factor.shape, f32),
            jax.ShapeDtypeStruct(channel_factor.shape, f32),
        ),
        in_specs=[anywhere, anywhere, vmem, vmem],
        out_specs=(anywhere, vmem),
        scratch_shapes=[
            pltpu.VMEM((groups, halves, chans, SUB, LANES), f32),
            pltpu.VMEM((groups, halves, rank, SUB, LANES), f32),
            pltpu.VMEM((rows, rank + chans, cols), jnp.bfloat16),
            pltpu.VMEM((rows, rank + chans, cols), jnp.bfloat16),
            pltpu.VMEM((n_ch - 1, halves, chans, SUB, LANES), f32),
            pltpu.VMEM((n_col, share, rank + chans), f32),
            pltpu.VMEM((n_col - 1, share, rank + chans), f32),
            pltpu.VMEM((n_row, share, rank + chans), f32),
            pltpu.VMEM((n_ch, n_col, share, chans), f32),
            pltpu.VMEM((n_ch, rows, rank, cols), f32),
            pltpu.VMEM((rows, rank, cols), f32),
            pltpu.VMEM((tall, rank, wide), f32),
            pltpu.VMEM((rows, rank, LANES), f32),
            pltpu.VMEM((rows, rank, LANES), f32),
            pltpu.VMEM((tall, SUB, wide), f32),
            pltpu.VMEM((rows, SUB, LANES), f32),
            pltpu.VMEM((rows, SUB, LANES), f32),
            pltpu.VMEM((tall, 5, SUB, wide), f32),
            pltpu.VMEM((tall, rank, wide), f32),
            pltpu.VMEM((tall, rank, wide), f32),
            pltpu.VMEM((rows, rank, cols), f32),
            dma((2, halves, groups)),
            dma((n_ch - 1, halves)), dma((n_ch - 1, halves)),
            dma((n_col - 1,)), dma((n_col - 1,)),
            dma((n_row - 1,)), dma((n_row - 1,)),
            dma((n_col * n_ch - 1,)), dma((n_col * n_ch - 1,)),
            dma((n_ch - 1, pieces)), dma((n_ch - 1, pieces)),
            dma((2, pieces + 1)), dma((2, pieces + 1)),
            dma((2,)), dma((2,)),
            dma((4,)), dma((4,)),
            dma((rows,)),
        ],
        compiler_params=pltpu.CompilerParams(
            collective_id=0, has_side_effects=True, vmem_limit_bytes=60 * 1024 * 1024
        ),
        name="factor",
    )(spectra, pixel_factor, channel_factor, labels)


def solution(mesh):
    sizes = tuple(mesh.shape[a] for a in ("row", "col", "ch"))
    placed = (P("ch", "row", "col"), P(None, "row", "col"), P(None, "ch"), P("row", "col"))
    return jax.shard_map(
        functools.partial(shards, sizes),
        mesh=mesh,
        in_specs=placed,
        out_specs=(P(None, "row", "col"), P(None, "ch")),
        check_vma=False,
    )
```

time: 81.9 us -> 78.8 us (0.962)
  Pallas kernels: 77.2 us -> 74.1 us
    pallas_call x1, Pallas kernels: 77.2 us -> 74.1 us  [shards(): pl.pallas_call(functools.partial(factor_kernel, sizes), out_shape=(jax.Sh...]
where the time goes in v1:
time: 78.8 us; the launch traced here: 78.6 us
  Pallas kernels  74.1 us (94%)
  local copies, waits for them, and re-layouts  3.82 us (5%)
    pallas_call x1, Pallas kernels, shards(): pl.pallas_call(functools.partial(factor_kernel, sizes), out_shape=(jax.Sh...  74.1 us
    unnamed x4, local copies, waits for them, and re-layouts  3.82 us

profile of v1, /device:TPU:1, one launch (start us, length us, event | category | flops | bytes accessed | tf_op | source)
XLA Modules:
  0.0 78.6 jit_solution(9710882206427904509)
XLA Ops:
  0.6 74.1 %factor.1 = (f32[64,32,256]{2,1,0:T(8,128)}, f32[64,192]{1,0:T(8,128)}) custom-call(f32[192,32,256]{2,1,0:T(8,128)} %x_hbm.1, f32[64,32,256]{2,1,0:T(8,128)} %w_hbm.1, f32[64,192]{1,0:T(8,128)} %cf_ref.1, s32[32,256]{1,0:T(8,128)} %lab_ref.1), custom_call_target="tpu_custom_call" | custom-call | tf_op jit(solution)/shard_map/factor/pallas_call | solution.py:580
  74.8 0.0 copy-start
  74.8 3.2 %copy.8 = f32[64,32,256]{2,1,0:T(8,128)} copy(f32[64,32,256]{2,1,0:T(8,128)} %get-tuple-element.4) | data formatting | bytes 4194304
  78.0 0.0 copy-done
  78.0 0.6 copy.9
Async XLA Ops:
  74.8 3.2 %copy-start = (f32[64,192]{1,0:T(8,128)S(1)}, f32[64,192]{1,0:T(8,128)}, u32[]{:S(2)}) copy-start(f32[64,192]{1,0:T(8,128)} %get-tuple-element.5) | copy-start | bytes 147460

commit v2 on v1

--- a/solution.py
+++ b/solution.py
@@ -14,6 +14,7 @@
 CHUNK = 2
 EARLY = 3
 BAND = 8
+LAG = 6
 
 epsilon = 1e-09
 
@@ -41,11 +42,11 @@
 
 
 def factor_kernel(
-    sizes, x_hbm, w_hbm, cf_ref, lab_ref, out_hbm, nc_out,
-    xs, ws, high, low, other, gram, gram_in, gram_row, nc, part, scale, field, left, right,
-    mark, mark_left, mark_right, weight, first, second, done,
+    sizes, x_hbm, w_hbm, cf_hbm, lab_hbm, done, nc_out,
+    cf_ref, lab_ref, xs, ws, high, low, other, gram, gram_in, gram_row, nc, part, scale, field, left, right,
+    mark, mark_left, mark_right, weight, first, second,
     load_sem, e_send, e_recv, g_send, g_recv, z_send, z_recv, n_send, n_recv,
-    t_send, t_recv, c_send, c_recv, r_send, r_recv, m_send, m_recv, out_sem,
+    t_send, t_recv, c_send, c_recv, r_send, r_recv, m_send, m_recv, small_sem,
 ):
     n_row, n_col, n_ch = sizes
     rank, rows, cols = w_hbm.shape
@@ -83,10 +84,6 @@
             axis=1,
         )
 
-    for g in range(groups):
-        for copy in load(g):
-            copy.start()
-
     barrier = pltpu.get_barrier_semaphore()
     for d in range(1, n_row):
         pl.semaphore_signal(
@@ -96,30 +93,6 @@
         pl.semaphore_signal(
             barrier, inc=1, device_id=side(me_col, me_ch, d, n_col, n_ch), device_id_type=MESH
         )
-
-    for buffer, edge in (
-        (left, 0), (mark_left, 0), (right, n_col - 1), (mark_right, n_col - 1),
-    ):
-
-        @pl.when(me_col == edge)
-        def _():
-            buffer[...] = jnp.zeros_like(buffer)
-
-    for at, edge in ((0, 0), (rows + SMOOTH, n_row - 1)):
-        for buffer in (field, mark):
-
-            @pl.when(me_row == edge)
-            def _():
-                buffer[pl.ds(at, SMOOTH)] = jnp.zeros((SMOOTH,) + buffer.shape[1:], jnp.float32)
-
-    def marks(r, carry):
-        row = (lab_ref[pl.ds(r, 1), :] + 1).astype(jnp.float32)
-        mark[r + SMOOTH, :, pl.ds(0, cols)] = jnp.broadcast_to(row, (SUB, cols))
-        return carry
-
-    lax.fori_loop(0, rows, marks, 0)
-
-    gram[...] = jnp.zeros_like(gram)
 
     def to_early(d, h):
         return pltpu.make_async_remote_copy(
@@ -184,10 +157,46 @@
         def _():
             copy(-1).wait_send()
 
+    for copy in load(0):
+        copy.start()
+    lab_load = pltpu.make_async_copy(lab_hbm, lab_ref, small_sem.at[0])
+    cf_load = pltpu.make_async_copy(cf_hbm, cf_ref, small_sem.at[1])
+    lab_load.start()
     pl.semaphore_wait(barrier, n_row - 1 + n_col * n_ch - 1)
     for d in range(1, n_ch):
         for h in range(halves):
             to_early(d, h).start()
+    for g in range(1, groups):
+        for copy in load(g):
+            copy.start()
+    cf_load.start()
+
+    for buffer, edge in (
+        (left, 0), (mark_left, 0), (right, n_col - 1), (mark_right, n_col - 1),
+    ):
+
+        @pl.when(me_col == edge)
+        def _():
+            buffer[...] = jnp.zeros_like(buffer)
+
+    for at, edge in ((0, 0), (rows + SMOOTH, n_row - 1)):
+        for buffer in (field, mark):
+
+            @pl.when(me_row == edge)
+            def _():
+                buffer[pl.ds(at, SMOOTH)] = jnp.zeros((SMOOTH,) + buffer.shape[1:], jnp.float32)
+
+    lab_load.wait()
+
+    def marks(r, carry):
+        row = (lab_ref[pl.ds(r, 1), :] + 1).astype(jnp.float32)
+        mark[r + SMOOTH, :, pl.ds(0, cols)] = jnp.broadcast_to(row, (SUB, cols))
+        return carry
+
+    lax.fori_loop(0, rows, marks, 0)
+
+    gram[...] = jnp.zeros_like(gram)
+
     start_pair(mark_side, me_col, n_col)
 
     def gather(g, carry):
@@ -267,6 +276,7 @@
         return carry
 
     lax.fori_loop(1, tall - 1, coefficients, 0)
+    cf_load.wait()
 
     for d in range(1, n_row):
         from_row(d).wait_recv()
@@ -433,9 +443,6 @@
         total = total + weight[e, 4] * pltpu.roll(here, wide - 1, 2)
         return total.reshape(band[1], wide)
 
-    def put(r):
-        return pltpu.make_async_copy(done.at[r], out_hbm.at[:, r, :], out_sem.at[r])
-
     def one(e, band=every):
         first[e, pl.ds(*band), :] = smooth(field, e, band)
 
@@ -443,14 +450,14 @@
         second[e, pl.ds(*band), :] = smooth(first, e, band)
 
     def three(e, band=every):
-        done[e - SMOOTH, pl.ds(*band), :] = smooth(second, e, band)[:, :cols]
-
-    def three_put(e):
-        three(e)
-        put(e - SMOOTH).start()
+        value = smooth(second, e, band)
+        for h in range(halves):
+            rows_of = done.at[h].reshape(rank * rows, LANES)
+            start = band[0] * rows + e - SMOOTH
+            rows_of[pl.ds(start, band[1], stride=rows), :] = value[:, h * LANES:(h + 1) * LANES]
 
     def sweep(starts, counts):
-        for stage, start, count in zip((one, two, three_put), starts, counts):
+        for stage, start, count in zip((one, two, three), starts, counts):
             def step(k, carry, f=stage, s=start):
                 f(s + k)
                 return carry
@@ -510,16 +517,22 @@
     widen_chunk(chunks - 1)
     sweep_chunk(chunks - 1)
 
-    def band_step(q, carry):
-        finish_band(q - 2)
+    def rise(q, carry):
         raise_band(q)
         return carry
 
-    lax.fori_loop(2, bands, band_step, 0)
-    for q in (bands - 2, bands - 1):
+    def rise_and_finish(q, carry):
+        raise_band(q)
+        finish_band(q - LAG)
+        return carry
+
+    def finish(q, carry):
         finish_band(q)
-    for e in range(main, min(edge + 3, last)):
-        put(e - SMOOTH).start()
+        return carry
+
+    lax.fori_loop(2, LAG, rise, 0)
+    lax.fori_loop(LAG, bands, rise_and_finish, 0)
+    lax.fori_loop(bands - LAG, bands, finish, 0)
 
     for d in range(1, n_col):
         to_col(d).wait_send()
@@ -551,11 +564,16 @@
         for h in range(halves):
             to_early(d, h).wait_send()
 
-    def drain_out(r, carry):
-        put(r).wait()
-        return carry
-
-    lax.fori_loop(0, rows, drain_out, 0)
+
+def store_kernel(done, new_channel, out_hbm, nc_hbm, sem):
+    copies = [pltpu.make_async_copy(new_channel, nc_hbm, sem.at[0])]
+    for h in range(done.shape[0]):
+        target = out_hbm.at[:, :, pl.ds(h * LANES, LANES)]
+        copies.append(pltpu.make_async_copy(done.at[h], target, sem.at[h + 1]))
+    for copy in copies:
+        copy.start()
+    for copy in copies:
+        copy.wait()
 
 
 def side(me_col, me_ch, d, n_col, n_ch):
@@ -574,18 +592,20 @@
     wide = cols + LANES
     halves, groups = cols // LANES, rows // SUB
     f32 = jnp.float32
-    vmem = pl.BlockSpec(memory_space=pltpu.VMEM)
     anywhere = pl.BlockSpec(memory_space=pl.ANY)
     dma = pltpu.SemaphoreType.DMA
-    return pl.pallas_call(
+    kept = pl.BlockSpec(memory_space=pltpu.VMEM)
+    done, new_channel = pl.pallas_call(
         functools.partial(factor_kernel, sizes),
         out_shape=(
-            jax.ShapeDtypeStruct(pixel_factor.shape, f32),
-            jax.ShapeDtypeStruct(channel_factor.shape, f32),
+            pltpu.VMEM((halves, rank, rows, LANES), f32),
+            pltpu.VMEM(channel_factor.shape, f32),
         ),
-        in_specs=[anywhere, anywhere, vmem, vmem],
-        out_specs=(anywhere, vmem),
+        in_specs=[anywhere] * 4,
+        out_specs=(kept, kept),
         scratch_shapes=[
+            pltpu.VMEM(channel_factor.shape, f32),
+            pltpu.VMEM(labels.shape, labels.dtype),
             pltpu.VMEM((groups, halves, chans, SUB, LANES), f32),
             pltpu.VMEM((groups, halves, rank, SUB, LANES), f32),
             pltpu.VMEM((rows, rank + chans, cols), jnp.bfloat16),
@@ -606,7 +626,6 @@
             pltpu.VMEM((tall, 5, SUB, wide), f32),
             pltpu.VMEM((tall, rank, wide), f32),
             pltpu.VMEM((tall, rank, wide), f32),
-            pltpu.VMEM((rows, rank, cols), f32),
             dma((2, halves, groups)),
             dma((n_ch - 1, halves)), dma((n_ch - 1, halves)),
             dma((n_col - 1,)), dma((n_col - 1,)),
@@ -616,13 +635,25 @@
             dma((2, pieces + 1)), dma((2, pieces + 1)),
             dma((2,)), dma((2,)),
             dma((4,)), dma((4,)),
-            dma((rows,)),
+            dma((2,)),
         ],
         compiler_params=pltpu.CompilerParams(
-            collective_id=0, has_side_effects=True, vmem_limit_bytes=60 * 1024 * 1024
+            collective_id=0, has_side_effects=True, vmem_limit_bytes=52 * 1024 * 1024
         ),
         name="factor",
     )(spectra, pixel_factor, channel_factor, labels)
+    return pl.pallas_call(
+        store_kernel,
+        out_shape=(
+            jax.ShapeDtypeStruct(pixel_factor.shape, f32),
+            jax.ShapeDtypeStruct(channel_factor.shape, f32),
+        ),
+        in_specs=[kept, kept],
+        out_specs=(anywhere, anywhere),
+        scratch_shapes=[dma((halves + 1,))],
+        compiler_params=pltpu.CompilerParams(vmem_limit_bytes=4 * 1024 * 1024),
+        name="store",
+    )(done, new_channel)
 
 
 def solution(mesh):

time: 78.8 us -> 69.7 us (0.88)
  Pallas kernels: 74.1 us -> 68.5 us
  local copies, waits for them, and re-layouts: 3.82 us -> 0 us
    pallas_call x1 -> x2, Pallas kernels: 74.1 us -> 68.5 us  [the longest x1 67.2 us: shards(): pl.pallas_call(functools.partial(factor_kernel, sizes), out_shape=(pltpu....]
    unnamed x4 -> x0, local copies, waits for them, and re-layouts: 3.82 us -> none
where the time goes in v2:
time: 69.7 us; the launch traced here: 69.2 us
  Pallas kernels  68.5 us (98%)
    pallas_call x1, Pallas kernels, shards(): pl.pallas_call(functools.partial(factor_kernel, sizes), out_shape=(pltpu....  67.2 us

profile of v2, /device:TPU:1, one launch (start us, length us, event | category | flops | bytes accessed | tf_op | source)
XLA Modules:
  0.0 69.2 jit_solution(10835804314956348558)
XLA Ops:
  0.6 67.2 %factor.1 = (f32[2,64,32,128]{3,2,1,0:T(8,128)S(1)}, f32[64,192]{1,0:T(8,128)S(1)}) custom-call(f32[192,32,256]{2,1,0:T(8,128)} %x_hbm.1, f32[64,32,256]{2,1,0:T(8,128)} %w_hbm.1, f32[64,192]{1,0:T(8,128)} %cf_hbm.1, s32[32,256]{1,0:T(8,128)} %lab_hbm.1), custom_call_target="tpu_custom_call" | custom-call | tf_op jit(solution)/shard_map/factor/pallas_call | solution.py:598
  67.8 1.4 %store.1 = (f32[64,32,256]{2,1,0:T(8,128)}, f32[64,192]{1,0:T(8,128)}) custom-call(f32[2,64,32,128]{3,2,1,0:T(8,128)S(1)} %get-tuple-element.4.done, f32[64,192]{1,0:T(8,128)S(1)} %get-tuple-element.5.new_channel), custom_call_target="tpu_custom_call" | custom-call | tf_op jit(solution)/shard_map/store/pallas_call | solution.py:645

commit v3 on v2

--- a/solution.py
+++ b/solution.py
@@ -13,8 +13,7 @@
 SUB = 8
 CHUNK = 2
 EARLY = 3
-BAND = 8
-LAG = 6
+BAND = 32
 
 epsilon = 1e-09
 
@@ -41,9 +40,24 @@
 NN = ((1,), (0,))
 
 
+def each(start, count, width, act):
+    def body(i, carry):
+        for k in range(width):
+            act(start + i * width + k)
+        return carry
+
+    whole = count // width
+    if whole == 1:
+        body(0, 0)
+    elif whole:
+        lax.fori_loop(0, whole, body, 0)
+    for k in range(whole * width, count):
+        act(start + k)
+
+
 def factor_kernel(
     sizes, x_hbm, w_hbm, cf_hbm, lab_hbm, done, nc_out,
-    cf_ref, lab_ref, xs, ws, high, low, other, gram, gram_in, gram_row, nc, part, scale, field, left, right,
+    cf_ref, lab_ref, xs, ws, high, low, other, gram, gram_in, gram_row, nc, part, scale, field, sides,
     mark, mark_left, mark_right, weight, first, second,
     load_sem, e_send, e_recv, g_send, g_recv, z_send, z_recv, n_send, n_recv,
     t_send, t_recv, c_send, c_recv, r_send, r_recv, m_send, m_recv, small_sem,
@@ -89,9 +103,13 @@
         pl.semaphore_signal(
             barrier, inc=1, device_id={"row": lax.rem(me_row + d, n_row)}, device_id_type=MESH
         )
-    for d in range(1, n_col * n_ch):
+    for d in range(1, n_col):
         pl.semaphore_signal(
-            barrier, inc=1, device_id=side(me_col, me_ch, d, n_col, n_ch), device_id_type=MESH
+            barrier, inc=1, device_id={"col": lax.rem(me_col + d, n_col)}, device_id_type=MESH
+        )
+    for d in range(1, n_ch):
+        pl.semaphore_signal(
+            barrier, inc=1, device_id={"ch": lax.rem(me_ch + d, n_ch)}, device_id_type=MESH
         )
 
     def to_early(d, h):
@@ -157,27 +175,27 @@
         def _():
             copy(-1).wait_send()
 
-    for copy in load(0):
+    for copy in (*load(0), *load(1)):
         copy.start()
     lab_load = pltpu.make_async_copy(lab_hbm, lab_ref, small_sem.at[0])
     cf_load = pltpu.make_async_copy(cf_hbm, cf_ref, small_sem.at[1])
     lab_load.start()
-    pl.semaphore_wait(barrier, n_row - 1 + n_col * n_ch - 1)
+    cf_load.start()
+    pl.semaphore_wait(barrier, n_row + n_col + n_ch - 3)
     for d in range(1, n_ch):
         for h in range(halves):
             to_early(d, h).start()
-    for g in range(1, groups):
+    for g in range(2, groups):
         for copy in load(g):
             copy.start()
-    cf_load.start()
 
     for buffer, edge in (
-        (left, 0), (mark_left, 0), (right, n_col - 1), (mark_right, n_col - 1),
+        (sides.at[0], 0), (mark_left, 0), (sides.at[1], n_col - 1), (mark_right, n_col - 1),
     ):
 
         @pl.when(me_col == edge)
         def _():
-            buffer[...] = jnp.zeros_like(buffer)
+            buffer[...] = jnp.zeros(buffer.shape, jnp.float32)
 
     for at, edge in ((0, 0), (rows + SMOOTH, n_row - 1)):
         for buffer in (field, mark):
@@ -188,12 +206,11 @@
 
     lab_load.wait()
 
-    def marks(r, carry):
+    def marks(r):
         row = (lab_ref[pl.ds(r, 1), :] + 1).astype(jnp.float32)
         mark[r + SMOOTH, :, pl.ds(0, cols)] = jnp.broadcast_to(row, (SUB, cols))
-        return carry
-
-    lax.fori_loop(0, rows, marks, 0)
+
+    each(0, rows, 8, marks)
 
     gram[...] = jnp.zeros_like(gram)
 
@@ -218,7 +235,7 @@
     def to_col(d):
         peer = lax.rem(me_col + d, n_col)
         return pltpu.make_async_remote_copy(
-            gram.at[peer], gram_in.at[d - 1], g_send.at[d - 1], g_recv.at[d - 1],
+            gram.at[peer], gram_in.at[d - 1], g_send.at[0], g_recv.at[d - 1],
             device_id={"col": peer}, device_id_type=MESH,
         )
 
@@ -245,14 +262,14 @@
     def to_row(d):
         peer = lax.rem(me_row + d, n_row)
         return pltpu.make_async_remote_copy(
-            gram_row.at[me_row], gram_row.at[me_row], z_send.at[d - 1], z_recv.at[d - 1],
+            gram_row.at[me_row], gram_row.at[me_row], z_send.at[0], z_recv.at[d - 1],
             device_id={"row": peer}, device_id_type=MESH,
         )
 
     def from_row(d):
         peer = lax.rem(me_row + n_row - d, n_row)
         return pltpu.make_async_remote_copy(
-            gram_row.at[peer], gram_row.at[peer], z_send.at[d - 1], z_recv.at[d - 1],
+            gram_row.at[peer], gram_row.at[peer], z_send.at[0], z_recv.at[d - 1],
             device_id={"row": peer}, device_id_type=MESH,
         )
 
@@ -261,7 +278,7 @@
 
     receive_pair(mark_across, me_row, n_row)
 
-    def coefficients(e, carry):
+    def coefficients(e):
         center = mark[e]
         around = (
             mark[e - 1], mark[e + 1], pltpu.roll(center, 1, 1), pltpu.roll(center, wide - 1, 1)
@@ -273,9 +290,8 @@
         weight[e, 0] = own_scale
         for j in range(4):
             weight[e, j + 1] = parts[j] * own_scale
-        return carry
-
-    lax.fori_loop(1, tall - 1, coefficients, 0)
+
+    each(1, tall - 2, 4, coefficients)
     cf_load.wait()
 
     for d in range(1, n_row):
@@ -290,26 +306,32 @@
     own_cf = cf_ref[pl.ds(pl.multiple_of(me_col * share, share), share), :]
     nc[me_ch, me_col] = own_cf * total[:, rank:] / (under + epsilon)
 
-    def to_side(d):
-        return pltpu.make_async_remote_copy(
-            nc.at[me_ch, me_col], nc.at[me_ch, me_col], n_send.at[d - 1], n_recv.at[d - 1],
-            device_id=side(me_col, me_ch, d, n_col, n_ch), device_id_type=MESH,
-        )
-
-    def from_side(d):
-        at = side(me_col, me_ch, n_col * n_ch - d, n_col, n_ch)
-        slot = nc.at[at["ch"], at["col"]]
-        return pltpu.make_async_remote_copy(
-            slot, slot, n_send.at[d - 1], n_recv.at[d - 1],
-            device_id=at, device_id_type=MESH,
-        )
-
-    same = [d for d in range(1, n_col * n_ch) if d % n_ch == 0]
-    away = [d for d in range(1, n_col * n_ch) if d % n_ch]
-    for d in same + away:
-        to_side(d).start()
-    for d in same:
-        from_side(d).wait_recv()
+    def spread(d, back, h, k):
+        col = lax.rem(me_col + (n_col - d if back else 0), n_col)
+        slot = nc.at[h, col]
+        return pltpu.make_async_remote_copy(
+            slot, slot, n_send.at[k], n_recv.at[k],
+            device_id={"col": lax.rem(me_col + d, n_col)}, device_id_type=MESH,
+        )
+
+    def cross(d, back):
+        slot = nc.at[lax.rem(me_ch + (n_ch - d if back else 0), n_ch), me_col]
+        k = n_col - 1 + d - 1
+        return pltpu.make_async_remote_copy(
+            slot, slot, n_send.at[k], n_recv.at[k],
+            device_id={"ch": lax.rem(me_ch + d, n_ch)}, device_id_type=MESH,
+        )
+
+    def pass_on(d, c, back):
+        k = n_col - 1 + n_ch - 1 + (d - 1) * (n_col - 1) + c - 1
+        return spread(c, back, lax.rem(me_ch + n_ch - d, n_ch), k)
+
+    for c in range(1, n_col):
+        spread(c, False, me_ch, c - 1).start()
+    for d in range(1, n_ch):
+        cross(d, False).start()
+    for c in range(1, n_col):
+        spread(c, True, me_ch, c - 1).wait_recv()
 
     mine = nc[me_ch].reshape(rank, chans)
     nc_out[...] = mine
@@ -331,15 +353,28 @@
 
     def part_copy(d, peer, slot, k):
         return pltpu.make_async_remote_copy(
-            slot, slot, t_send.at[d - 1, k], t_recv.at[d - 1, k],
+            slot, slot, t_send.at[d - 1], t_recv.at[d - 1, k],
             device_id={"ch": peer}, device_id_type=MESH,
         )
 
     def chunk_slot(h, c):
         return part.at[h, pl.ds(c * CHUNK, CHUNK)]
 
-    def band_slot(h, q):
-        return part.at[h, pl.ds(main, tip), pl.ds(pl.multiple_of(q * BAND, BAND), BAND)]
+    odd = lax.rem(me_col, 2)
+
+    def lanes_of(phase):
+        if phase == 0:
+            return pl.ds(pl.multiple_of(odd * (cols - LANES), LANES), LANES)
+        return pl.ds(pl.multiple_of((1 - odd) * LANES, LANES), cols - LANES)
+
+    def piece_slot(phase):
+        def slot(h, q):
+            band = pl.ds(pl.multiple_of(q * BAND, BAND), BAND)
+            return part.at[h, pl.ds(main, tip), band, lanes_of(phase)]
+        return slot
+
+    def piece(phase, q):
+        return chunks + phase * bands + q
 
     def to_ch(d, slot, i, k):
         return part_copy(d, lax.rem(me_ch + d, n_ch), slot(me_ch, i), k)
@@ -348,22 +383,28 @@
         peer = lax.rem(me_ch + n_ch - d, n_ch)
         return part_copy(d, peer, slot(peer, i), k)
 
-    def send_part(c, carry):
+    def send_part(c):
         for k in range(CHUNK):
             own_part(c * CHUNK + k)
         for d in range(1, n_ch):
             to_ch(d, chunk_slot, c, c).start()
-        return carry
-
-    lax.fori_loop(0, chunks, send_part, 0)
+
+    each(0, chunks // 2, 2, send_part)
+    for d in range(1, n_ch):
+        cross(d, True).wait_recv()
+        for c in range(1, n_col):
+            pass_on(d, c, False).start()
+    each(chunks // 2, chunks - chunks // 2, 2, send_part)
     for r in range(main, early):
         own_part(r)
-    for q in range(bands):
-        for d in range(1, n_ch):
-            to_ch(d, band_slot, q, chunks + q).start()
-
-    for d in away:
-        from_side(d).wait_recv()
+    for phase in range(2):
+        for q in range(bands):
+            for d in range(1, n_ch):
+                to_ch(d, piece_slot(phase), q, piece(phase, q)).start()
+
+    for d in range(1, n_ch):
+        for c in range(1, n_col):
+            pass_on(d, c, True).wait_recv()
 
     def channel_gram(h):
         block = nc[h].reshape(rank, chans)
@@ -377,15 +418,13 @@
         cg = cg + channel_gram(h)
     cg = stacked(cg)
 
-    def scales(r, carry):
+    def scale_row(r):
         g, s = r // SUB, lax.rem(r, SUB)
         below = product(cg, high[r, pl.ds(0, rank), :], low[r, pl.ds(0, rank), :])
         scale[r] = image_row(ws.at[g], s) / (below + epsilon)
-        return carry
-
-    lax.fori_loop(0, rows, scales, 0)
 
     for r in range(early, rows):
+        scale_row(r)
         own_part(r)
     for d in range(1, n_ch):
         peer = lax.rem(me_ch + n_ch - d, n_ch)
@@ -399,12 +438,12 @@
 
     def field_side(start, count, band, k):
         def copy(step):
-            j, lanes, target = ((0, cols - LANES, left), (1, 0, right))[step < 0]
+            j, lanes = ((0, cols - LANES), (1, 0))[step < 0]
             return beside(
                 step,
                 field.at[pl.ds(start + SMOOTH, count), pl.ds(*band), pl.ds(lanes, LANES)],
-                target.at[pl.ds(start, count), pl.ds(*band)],
-                (c_send.at[j, k], c_recv.at[j, k]),
+                sides.at[j, pl.ds(start, count), pl.ds(*band)],
+                (c_send.at[j], c_recv.at[j, k]),
             )
         return copy
 
@@ -418,14 +457,19 @@
 
     def widen_rows(start, count, band, k):
         receive_pair(field_side(start, count, band, k), me_col, n_col)
+        join_rows(start, count, band)
+
+    def join_rows(start, count, band):
         at = (pl.ds(start, count), pl.ds(*band))
         shape = (count * band[1] // SUB, SUB, LANES)
-        edge = joined(left[at].reshape(shape), right[at].reshape(shape))
+        edge = joined(sides[(0,) + at].reshape(shape), sides[(1,) + at].reshape(shape))
         field[pl.ds(start + SMOOTH, count), pl.ds(*band), pl.ds(cols, LANES)] = edge.reshape(
             count, band[1], LANES
         )
 
     def raise_chunk(c):
+        for k in range(CHUNK):
+            scale_row(c * CHUNK + k)
         for d in range(1, n_ch):
             from_ch(d, chunk_slot, c, c).wait_recv()
         raise_rows(c * CHUNK, CHUNK, every, c)
@@ -452,22 +496,21 @@
     def three(e, band=every):
         value = smooth(second, e, band)
         for h in range(halves):
-            rows_of = done.at[h].reshape(rank * rows, LANES)
-            start = band[0] * rows + e - SMOOTH
-            rows_of[pl.ds(start, band[1], stride=rows), :] = value[:, h * LANES:(h + 1) * LANES]
+            lines = done.at[h, (e - SMOOTH) // SUB].reshape(rank * SUB, LANES)
+            start = band[0] * SUB + lax.rem(e - SMOOTH, SUB)
+            lines[pl.ds(start, band[1], stride=SUB), :] = value[:, h * LANES:(h + 1) * LANES]
 
     def sweep(starts, counts):
         for stage, start, count in zip((one, two, three), starts, counts):
-            def step(k, carry, f=stage, s=start):
-                f(s + k)
-                return carry
-            lax.fori_loop(0, count, step, 0)
+            each(start, count, 2, stage)
 
     def sweep_chunk(c):
         sweep((CHUNK * c + 2, CHUNK * c + 1, CHUNK * c), (CHUNK,) * 3)
 
+    at_end = chunks + 2 * bands
+    edge = early + SMOOTH
+    last = rows + SMOOTH
     near = -(-SMOOTH // CHUNK)
-    at_end = chunks + bands
     raise_rows(early, EARLY, every, at_end)
     for c in range(near):
         raise_chunk(c)
@@ -477,12 +520,37 @@
     start_pair(field_across, me_row, n_row)
     for c in range(near, near + 2):
         raise_chunk(c)
-    receive_pair(field_across, me_row, n_row)
-    edge = early + SMOOTH
-    last = rows + SMOOTH
-    sweep((edge + 1, edge + 2, edge + 3), (last + 1 - edge, last - 1 - edge, max(last - 3 - edge, 0)))
-    seen = near * CHUNK
-    sweep((1, 2, 3), (seen + 1, seen - 1, seen - 3))
+    for r in range(main, early):
+        scale_row(r)
+
+    def follow(c):
+        ends = [CHUNK * (c + 1) + SMOOTH - 1 - i for i in range(3)]
+        starts = [max(x - CHUNK, SMOOTH + 1 + i) for i, x in enumerate(ends)]
+        sweep(starts, [max(x - y, 0) for x, y in zip(ends, starts)])
+
+    for c in range(near):
+        follow(c)
+
+    gathered = gram_row.at[pl.ds(0, n_row - 1)]
+    pltpu.make_async_remote_copy(
+        gram_in, gram_in, g_send.at[0], g_recv.at[0],
+        device_id={"col": lax.rem(me_col + 1, n_col)}, device_id_type=MESH,
+    ).wait_send()
+    pltpu.make_async_remote_copy(
+        gathered, gathered, z_send.at[0], z_recv.at[0],
+        device_id={"row": lax.rem(me_row + 1, n_row)}, device_id_type=MESH,
+    ).wait_send()
+    for c in range(1, n_col):
+        spread(c, False, me_ch, c - 1).wait_send()
+    for d in range(1, n_ch):
+        cross(d, False).wait_send()
+        for c in range(1, n_col):
+            pass_on(d, c, False).wait_send()
+    for d in range(1, n_ch):
+        for h in range(halves):
+            to_early(d, h).wait_send()
+    sent_pair(mark_side, me_col, n_col)
+    sent_pair(mark_across, me_row, n_row)
 
     def step(c, carry):
         widen_chunk(c - 2)
@@ -490,19 +558,59 @@
         raise_chunk(c)
         return carry
 
-    lax.fori_loop(near + 2, chunks, step, 0)
+    clipped = -(-(SMOOTH + 3) // CHUNK) + 2
+    for c in range(near + 2, clipped):
+        widen_chunk(c - 2)
+        follow(c - 2)
+        raise_chunk(c)
+    middle = (clipped + chunks) // 2 - 1
+    lax.fori_loop(clipped, middle, step, 0)
+    receive_pair(field_across, me_row, n_row)
+    sweep((1, 2, 3), (SMOOTH,) * 3)
+    sweep((edge + 1, edge + 2, edge + 3), (last + 1 - edge, last - 1 - edge, max(last - 3 - edge, 0)))
+    lax.fori_loop(middle, chunks, step, 0)
+    sent_pair(field_across, me_row, n_row)
 
     def band_of(q):
         return (pl.multiple_of(q * BAND, BAND), BAND)
 
-    def raise_band(q):
+    def piece_side(phase, q, arriving):
+        to_right = odd if phase == 0 else 1 - odd
+        peer = me_col + 2 * to_right - 1
+        j = to_right if arriving else 1 - to_right
+        lanes = pl.ds(pl.multiple_of(to_right * (cols - LANES), LANES), LANES)
+        copy = pltpu.make_async_remote_copy(
+            field.at[pl.ds(main + SMOOTH, tip), pl.ds(*band_of(q)), lanes],
+            sides.at[j, pl.ds(main, tip), pl.ds(*band_of(q))],
+            c_send.at[j], c_recv.at[j, piece(phase, q)],
+            device_id={"col": lax.rem(peer + n_col, n_col)}, device_id_type=MESH,
+        )
+        return copy, jnp.logical_and(peer >= 0, peer < n_col)
+
+    def raise_piece(phase, q):
         for d in range(1, n_ch):
-            from_ch(d, band_slot, q, chunks + q).wait_recv()
-        raise_rows(main, tip, band_of(q), chunks + q)
+            from_ch(d, piece_slot(phase), q, piece(phase, q)).wait_recv()
+        at = (pl.ds(main, tip), pl.ds(*band_of(q)), lanes_of(phase))
+        top = part[(0,) + at]
+        for h in range(1, n_ch):
+            top = top + part[(h,) + at]
+        field[(pl.ds(main + SMOOTH, tip),) + at[1:]] = scale[at] * top
+        copy, there = piece_side(phase, q, False)
+
+        @pl.when(there)
+        def _():
+            copy.start()
 
     def finish_band(q):
         band = band_of(q)
-        widen_rows(main, tip, band, chunks + q)
+        for phase in range(2):
+            copy, there = piece_side(phase, q, True)
+
+            @pl.when(there)
+            def _():
+                copy.wait_recv()
+
+        join_rows(main, tip, band)
         for e in range(main + 2, edge + 1):
             one(e, band)
         for e in range(main + 1, edge + 2):
@@ -512,73 +620,46 @@
 
     widen_chunk(chunks - 2)
     sweep_chunk(chunks - 2)
-    for q in range(2):
-        raise_band(q)
-    widen_chunk(chunks - 1)
-    sweep_chunk(chunks - 1)
-
-    def rise(q, carry):
-        raise_band(q)
-        return carry
-
-    def rise_and_finish(q, carry):
-        raise_band(q)
-        finish_band(q - LAG)
-        return carry
+    def rise(phase):
+        def body(q, carry):
+            raise_piece(phase, q)
+            return carry
+        return body
 
     def finish(q, carry):
         finish_band(q)
         return carry
 
-    lax.fori_loop(2, LAG, rise, 0)
-    lax.fori_loop(LAG, bands, rise_and_finish, 0)
-    lax.fori_loop(bands - LAG, bands, finish, 0)
-
-    for d in range(1, n_col):
-        to_col(d).wait_send()
-    for d in range(1, n_row):
-        to_row(d).wait_send()
-    for d in range(1, n_col * n_ch):
-        to_side(d).wait_send()
-    sent_pair(mark_side, me_col, n_col)
-    sent_pair(mark_across, me_row, n_row)
-    sent_pair(field_across, me_row, n_row)
-    sent_pair(field_side(early, EARLY, every, at_end), me_col, n_col)
-
-    def drain_chunk(c, carry):
-        sent_pair(field_side(c * CHUNK, CHUNK, every, c), me_col, n_col)
-        for d in range(1, n_ch):
-            to_ch(d, chunk_slot, c, c).wait_send()
-        return carry
-
-    lax.fori_loop(0, chunks, drain_chunk, 0)
-
-    def drain_band(q, carry):
-        sent_pair(field_side(main, tip, band_of(q), chunks + q), me_col, n_col)
-        for d in range(1, n_ch):
-            to_ch(d, band_slot, q, chunks + q).wait_send()
-        return carry
-
-    lax.fori_loop(0, bands, drain_band, 0)
-    for d in range(1, n_ch):
-        for h in range(halves):
-            to_early(d, h).wait_send()
+    lax.fori_loop(0, bands, rise(0), 0)
+    widen_chunk(chunks - 1)
+    sweep_chunk(chunks - 1)
+    lax.fori_loop(0, bands, rise(1), 0)
+    lax.fori_loop(0, bands, finish, 0)
+    for d in range(1, n_ch):
+        whole = part.at[me_ch, pl.ds(0, early)]
+        pltpu.make_async_remote_copy(
+            whole, whole, t_send.at[d - 1], t_recv.at[d - 1, 0],
+            device_id={"ch": lax.rem(me_ch + d, n_ch)}, device_id_type=MESH,
+        ).wait_send()
+
+    def all_field_side(step):
+        j = int(step < 0)
+        return beside(step, sides.at[j], sides.at[j], (c_send.at[j], c_recv.at[j, 0]))
+
+    sent_pair(all_field_side, me_col, n_col)
 
 
 def store_kernel(done, new_channel, out_hbm, nc_hbm, sem):
     copies = [pltpu.make_async_copy(new_channel, nc_hbm, sem.at[0])]
-    for h in range(done.shape[0]):
-        target = out_hbm.at[:, :, pl.ds(h * LANES, LANES)]
-        copies.append(pltpu.make_async_copy(done.at[h], target, sem.at[h + 1]))
+    halves, groups = done.shape[:2]
+    for h in range(halves):
+        for g in range(groups):
+            target = out_hbm.at[:, pl.ds(g * SUB, SUB), pl.ds(h * LANES, LANES)]
+            copies.append(pltpu.make_async_copy(done.at[h, g], target, sem.at[len(copies)]))
     for copy in copies:
         copy.start()
     for copy in copies:
         copy.wait()
-
-
-def side(me_col, me_ch, d, n_col, n_ch):
-    place = lax.rem(me_col * n_ch + me_ch + d, n_col * n_ch)
-    return {"col": place // n_ch, "ch": lax.rem(place, n_ch)}
 
 
 def shards(sizes, spectra, pixel_factor, channel_factor, labels):
@@ -587,7 +668,7 @@
     chans = spectra.shape[0]
     share = rank // n_col
     early = rows - EARLY
-    pieces = (early - SMOOTH) // CHUNK + rank // BAND
+    pieces = (early - SMOOTH) // CHUNK + 2 * (rank // BAND)
     tall = rows + 2 * SMOOTH
     wide = cols + LANES
     halves, groups = cols // LANES, rows // SUB
@@ -598,7 +679,7 @@
     done, new_channel = pl.pallas_call(
         functools.partial(factor_kernel, sizes),
         out_shape=(
-            pltpu.VMEM((halves, rank, rows, LANES), f32),
+            pltpu.VMEM((halves, groups, rank, SUB, LANES), f32),
             pltpu.VMEM(channel_factor.shape, f32),
         ),
         in_specs=[anywhere] * 4,
@@ -618,8 +699,7 @@
             pltpu.VMEM((n_ch, rows, rank, cols), f32),
             pltpu.VMEM((rows, rank, cols), f32),
             pltpu.VMEM((tall, rank, wide), f32),
-            pltpu.VMEM((rows, rank, LANES), f32),
-            pltpu.VMEM((rows, rank, LANES), f32),
+            pltpu.VMEM((2, rows, rank, LANES), f32),
             pltpu.VMEM((tall, SUB, wide), f32),
             pltpu.VMEM((rows, SUB, LANES), f32),
             pltpu.VMEM((rows, SUB, LANES), f32),
@@ -628,11 +708,11 @@
             pltpu.VMEM((tall, rank, wide), f32),
             dma((2, halves, groups)),
             dma((n_ch - 1, halves)), dma((n_ch - 1, halves)),
-            dma((n_col - 1,)), dma((n_col - 1,)),
-            dma((n_row - 1,)), dma((n_row - 1,)),
+            dma((1,)), dma((n_col - 1,)),
+            dma((1,)), dma((n_row - 1,)),
             dma((n_col * n_ch - 1,)), dma((n_col * n_ch - 1,)),
-            dma((n_ch - 1, pieces)), dma((n_ch - 1, pieces)),
-            dma((2, pieces + 1)), dma((2, pieces + 1)),
+            dma((n_ch - 1,)), dma((n_ch - 1, pieces)),
+            dma((2,)), dma((2, pieces + 1)),
             dma((2,)), dma((2,)),
             dma((4,)), dma((4,)),
             dma((2,)),
@@ -650,7 +730,7 @@
         ),
         in_specs=[kept, kept],
         out_specs=(anywhere, anywhere),
-        scratch_shapes=[dma((halves + 1,))],
+        scratch_shapes=[dma((halves * groups + 1,))],
         compiler_params=pltpu.CompilerParams(vmem_limit_bytes=4 * 1024 * 1024),
         name="store",
     )(done, new_channel)

time: 69.7 us -> 67.8 us (0.973)
  Pallas kernels: 68.5 us -> 66.4 us
    pallas_call x1, Pallas kernels: 67.2 us -> 65 us  [shards(): pl.pallas_call(functools.partial(factor_kernel, sizes), out_shape=(pltpu....]
where the time goes in v3:
time: 67.8 us; the launch traced here: 67 us
  Pallas kernels  66.4 us (98%)
    pallas_call x1, Pallas kernels, shards(): pl.pallas_call(functools.partial(factor_kernel, sizes), out_shape=(pltpu....  65 us
    pallas_call x1, Pallas kernels, shards(): pl.pallas_call(store_kernel, out_shape=(jax.ShapeDtypeStruct(pixel_factor...  1.41 us

profile of v3, /device:TPU:1, one launch (start us, length us, event | category | flops | bytes accessed | tf_op | source)
XLA Modules:
  0.0 67.0 jit_solution(3491307797825775512)
XLA Ops:
  0.6 65.0 %factor.1 = (f32[2,4,64,8,128]{4,3,2,1,0:T(8,128)S(1)}, f32[64,192]{1,0:T(8,128)S(1)}) custom-call(f32[192,32,256]{2,1,0:T(8,128)} %x_hbm.1, f32[64,32,256]{2,1,0:T(8,128)} %w_hbm.1, f32[64,192]{1,0:T(8,128)} %cf_hbm.1, s32[32,256]{1,0:T(8,128)} %lab_hbm.1), custom_call_target="tpu_custom_call" | custom-call | tf_op jit(solution)/shard_map/factor/pallas_call | solution.py:679
  65.6 1.4 %store.1 = (f32[64,32,256]{2,1,0:T(8,128)}, f32[64,192]{1,0:T(8,128)}) custom-call(f32[2,4,64,8,128]{4,3,2,1,0:T(8,128)S(1)} %get-tuple-element.4.done, f32[64,192]{1,0:T(8,128)S(1)} %get-tuple-element.5.new_channel), custom_call_target="tpu_custom_call" | custom-call | tf_op jit(solution)/shard_map/store/pallas_call | solution.py:725

commit v4 on v3

--- a/solution.py
+++ b/solution.py
@@ -57,10 +57,10 @@
 
 def factor_kernel(
     sizes, x_hbm, w_hbm, cf_hbm, lab_hbm, done, nc_out,
-    cf_ref, lab_ref, xs, ws, high, low, other, gram, gram_in, gram_row, nc, part, scale, field, sides,
+    cf_ref, lab_ref, xs, ws, high, low, other, products, gram, gram_in, gram_row, nc, part, scale, field, sides,
     mark, mark_left, mark_right, weight, first, second,
     load_sem, e_send, e_recv, g_send, g_recv, z_send, z_recv, n_send, n_recv,
-    t_send, t_recv, c_send, c_recv, r_send, r_recv, m_send, m_recv, small_sem,
+    t_send, t_recv, c_send, c_recv, r_send, r_recv, m_send, m_recv, small_sem, relay,
 ):
     n_row, n_col, n_ch = sizes
     rank, rows, cols = w_hbm.shape
@@ -99,10 +99,35 @@
         )
 
     barrier = pltpu.get_barrier_semaphore()
-    for d in range(1, n_row):
+    def tell(step, semaphore):
         pl.semaphore_signal(
-            barrier, inc=1, device_id={"row": lax.rem(me_row + d, n_row)}, device_id_type=MESH
-        )
+            semaphore, inc=1, device_id={"row": lax.rem(me_row + n_row + step, n_row)},
+            device_id_type=MESH,
+        )
+
+    def told(step, k):
+        return relay.at[int(step < 0), k - 1]
+
+    def known(step, k):
+        return me_row >= k if step > 0 else me_row < n_row - k
+
+    def pass_greeting(k):
+        for step in (1, -1):
+            @pl.when(jnp.logical_and(known(step, k), known(-step, 1)))
+            def _():
+                tell(step, told(step, k))
+
+    def hear_greeting(k):
+        for step in (1, -1):
+            @pl.when(known(step, k + 1))
+            def _():
+                pl.semaphore_wait(told(step, k), 1)
+
+    for step in (1, -1):
+        @pl.when(known(-step, 1))
+        def _():
+            tell(step, barrier)
+
     for d in range(1, n_col):
         pl.semaphore_signal(
             barrier, inc=1, device_id={"col": lax.rem(me_col + d, n_col)}, device_id_type=MESH
@@ -175,17 +200,18 @@
         def _():
             copy(-1).wait_send()
 
-    for copy in (*load(0), *load(1)):
+    for copy in load(0):
         copy.start()
     lab_load = pltpu.make_async_copy(lab_hbm, lab_ref, small_sem.at[0])
     cf_load = pltpu.make_async_copy(cf_hbm, cf_ref, small_sem.at[1])
     lab_load.start()
     cf_load.start()
-    pl.semaphore_wait(barrier, n_row + n_col + n_ch - 3)
+    beside_me = (me_row > 0).astype(jnp.int32) + (me_row < n_row - 1).astype(jnp.int32)
+    pl.semaphore_wait(barrier, n_col + n_ch - 2 + beside_me)
     for d in range(1, n_ch):
         for h in range(halves):
             to_early(d, h).start()
-    for g in range(2, groups):
+    for g in range(1, groups):
         for copy in load(g):
             copy.start()
 
@@ -212,25 +238,40 @@
 
     each(0, rows, 8, marks)
 
-    gram[...] = jnp.zeros_like(gram)
+    products[...] = jnp.zeros_like(products)
 
     start_pair(mark_side, me_col, n_col)
+    if n_row > 2:
+        pass_greeting(1)
 
     def gather(g, carry):
         for copy in load(g):
             copy.wait()
-        upper = lower = 0.0
+        sums = [0.0, 0.0]
         for s in range(SUB):
             both = jnp.concatenate([image_row(ws.at[g], s), image_row(xs.at[g], s)], axis=0)
             h, l = split(both)
             high[g * SUB + s] = h
             low[g * SUB + s] = l
-            upper = upper + dot(jnp.concatenate([h[:rank], l[:rank]], axis=0), h, NT)
-            lower = lower + dot(h[:rank], l, NT)
-        gram[...] += (upper[:rank] + upper[rank:] + lower).reshape(gram.shape)
+            rows_of = jnp.concatenate([h, l[rank:]], axis=0)
+            sums[s % 2] = sums[s % 2] + dot(
+                rows_of, jnp.concatenate([h[:rank], l[:rank]], axis=0), NT
+            )
+        products[...] += sums[0] + sums[1]
         return carry
 
     lax.fori_loop(0, groups, gather, 0)
+
+    w_part = products[pl.ds(0, rank), :]
+    first_half = lax.broadcasted_iota(jnp.int32, (1, 2 * rank), 1) < rank
+    x_part = products[pl.ds(rank, chans), :] + jnp.where(
+        first_half, products[pl.ds(rank + chans, chans), :], 0.0
+    )
+    turned = jnp.concatenate([w_part, x_part], axis=0).T
+    turned = turned[:rank] + turned[rank:]
+    gram[...] = turned.reshape(gram.shape)
+    swapped = pltpu.roll(w_part, rank, 1)[:, :rank]
+    gram[:, :, pl.ds(0, rank)] += swapped.reshape(n_col, share, rank)
 
     def to_col(d):
         peer = lax.rem(me_col + d, n_col)
@@ -241,6 +282,10 @@
 
     for d in range(1, n_col):
         to_col(d).start()
+    for k in range(1, n_row - 1):
+        hear_greeting(k)
+        if k < n_row - 2:
+            pass_greeting(k + 1)
 
     lane = lax.broadcasted_iota(jnp.int32, (1, SUB, LANES), 2)
 
@@ -692,6 +737,7 @@
             pltpu.VMEM((rows, rank + chans, cols), jnp.bfloat16),
             pltpu.VMEM((rows, rank + chans, cols), jnp.bfloat16),
             pltpu.VMEM((n_ch - 1, halves, chans, SUB, LANES), f32),
+            pltpu.VMEM((rank + 2 * chans, 2 * rank), f32),
             pltpu.VMEM((n_col, share, rank + chans), f32),
             pltpu.VMEM((n_col - 1, share, rank + chans), f32),
             pltpu.VMEM((n_row, share, rank + chans), f32),
@@ -716,6 +762,7 @@
             dma((2,)), dma((2,)),
             dma((4,)), dma((4,)),
             dma((2,)),
+            pltpu.SemaphoreType.REGULAR((2, max(n_row - 2, 1))),
         ],
         compiler_params=pltpu.CompilerParams(
             collective_id=0, has_side_effects=True, vmem_limit_bytes=52 * 1024 * 1024

time: 67.8 us -> 67.1 us (0.990)
  no operation moved by 1% of the time
where the time goes in v4:
time: 67.1 us; the launch traced here: 66.4 us
  Pallas kernels  65.8 us (98%)
    pallas_call x1, Pallas kernels, shards(): pl.pallas_call(functools.partial(factor_kernel, sizes), out_shape=(pltpu....  64.4 us
    pallas_call x1, Pallas kernels, shards(): pl.pallas_call(store_kernel, out_shape=(jax.ShapeDtypeStruct(pixel_factor...  1.41 us

profile of v4, /device:TPU:1, one launch (start us, length us, event | category | flops | bytes accessed | tf_op | source)
XLA Modules:
  0.0 66.4 jit_solution(6985538577932435732)
XLA Ops:
  0.6 64.4 %factor.1 = (f32[2,4,64,8,128]{4,3,2,1,0:T(8,128)S(1)}, f32[64,192]{1,0:T(8,128)S(1)}) custom-call(f32[192,32,256]{2,1,0:T(8,128)} %x_hbm.1, f32[64,32,256]{2,1,0:T(8,128)} %w_hbm.1, f32[64,192]{1,0:T(8,128)} %cf_hbm.1, s32[32,256]{1,0:T(8,128)} %lab_hbm.1), custom_call_target="tpu_custom_call" | custom-call | tf_op jit(solution)/shard_map/factor/pallas_call | solution.py:724
  65.0 1.4 %store.1 = (f32[64,32,256]{2,1,0:T(8,128)}, f32[64,192]{1,0:T(8,128)}) custom-call(f32[2,4,64,8,128]{4,3,2,1,0:T(8,128)S(1)} %get-tuple-element.4.done, f32[64,192]{1,0:T(8,128)S(1)} %get-tuple-element.5.new_channel), custom_call_target="tpu_custom_call" | custom-call | tf_op jit(solution)/shard_map/store/pallas_call | solution.py:772

commit v5 on v4

--- a/solution.py
+++ b/solution.py
@@ -13,7 +13,8 @@
 SUB = 8
 CHUNK = 2
 EARLY = 3
-BAND = 32
+HALVES = 2
+BAND = 16
 
 epsilon = 1e-09
 
@@ -273,15 +274,21 @@
     swapped = pltpu.roll(w_part, rank, 1)[:, :rank]
     gram[:, :, pl.ds(0, rank)] += swapped.reshape(n_col, share, rank)
 
-    def to_col(d):
+    lines = share // HALVES
+
+    def half(k):
+        return pl.ds(k * lines, lines)
+
+    def to_col(d, k):
         peer = lax.rem(me_col + d, n_col)
         return pltpu.make_async_remote_copy(
-            gram.at[peer], gram_in.at[d - 1], g_send.at[0], g_recv.at[d - 1],
+            gram.at[peer, half(k)], gram_in.at[d - 1, half(k)], g_send.at[0], g_recv.at[d - 1, k],
             device_id={"col": peer}, device_id_type=MESH,
         )
 
-    for d in range(1, n_col):
-        to_col(d).start()
+    for k in range(HALVES):
+        for d in range(1, n_col):
+            to_col(d, k).start()
     for k in range(1, n_row - 1):
         hear_greeting(k)
         if k < n_row - 2:
@@ -298,28 +305,22 @@
     mark[pl.ds(SMOOTH, rows), :, pl.ds(cols, LANES)] = joined(mark_left[...], mark_right[...])
     start_pair(mark_across, me_row, n_row)
 
-    own = gram[me_col]
-    for d in range(1, n_col):
-        to_col(d).wait_recv()
-        own = own + gram_in[d - 1]
-    gram_row[me_row] = own
-
-    def to_row(d):
-        peer = lax.rem(me_row + d, n_row)
+    def along_row(d, back, k):
+        at = lax.rem(me_row + (n_row - d if back else 0), n_row)
+        slot = gram_row.at[at, half(k)]
         return pltpu.make_async_remote_copy(
-            gram_row.at[me_row], gram_row.at[me_row], z_send.at[0], z_recv.at[d - 1],
-            device_id={"row": peer}, device_id_type=MESH,
-        )
-
-    def from_row(d):
-        peer = lax.rem(me_row + n_row - d, n_row)
-        return pltpu.make_async_remote_copy(
-            gram_row.at[peer], gram_row.at[peer], z_send.at[0], z_recv.at[d - 1],
-            device_id={"row": peer}, device_id_type=MESH,
-        )
-
-    for d in range(1, n_row):
-        to_row(d).start()
+            slot, slot, z_send.at[0], z_recv.at[d - 1, k],
+            device_id={"row": lax.rem(me_row + d, n_row)}, device_id_type=MESH,
+        )
+
+    for k in range(HALVES):
+        own = gram[me_col, half(k)]
+        for d in range(1, n_col):
+            to_col(d, k).wait_recv()
+            own = own + gram_in[d - 1, half(k)]
+        gram_row[me_row, half(k)] = own
+        for d in range(1, n_row):
+            along_row(d, False, k).start()
 
     receive_pair(mark_across, me_row, n_row)
 
@@ -339,44 +340,51 @@
     each(1, tall - 2, 4, coefficients)
     cf_load.wait()
 
-    for d in range(1, n_row):
-        from_row(d).wait_recv()
-    total = gram_row[0]
-    for z in range(1, n_row):
-        total = total + gram_row[z]
-    under = jnp.dot(
-        total[:, :rank], cf_ref[...], precision=lax.Precision.HIGHEST,
-        preferred_element_type=jnp.float32,
-    )
-    own_cf = cf_ref[pl.ds(pl.multiple_of(me_col * share, share), share), :]
-    nc[me_ch, me_col] = own_cf * total[:, rank:] / (under + epsilon)
-
-    def spread(d, back, h, k):
+    def spread(d, back, h, k, part_of=slice(None)):
         col = lax.rem(me_col + (n_col - d if back else 0), n_col)
-        slot = nc.at[h, col]
+        slot = nc.at[h, col, part_of]
         return pltpu.make_async_remote_copy(
             slot, slot, n_send.at[k], n_recv.at[k],
             device_id={"col": lax.rem(me_col + d, n_col)}, device_id_type=MESH,
         )
 
+    def spread_half(c, back, k):
+        return spread(c, back, me_ch, (c - 1) * HALVES + k, half(k))
+
+    first_cross = (n_col - 1) * HALVES
+
     def cross(d, back):
         slot = nc.at[lax.rem(me_ch + (n_ch - d if back else 0), n_ch), me_col]
-        k = n_col - 1 + d - 1
+        k = first_cross + d - 1
         return pltpu.make_async_remote_copy(
             slot, slot, n_send.at[k], n_recv.at[k],
             device_id={"ch": lax.rem(me_ch + d, n_ch)}, device_id_type=MESH,
         )
 
     def pass_on(d, c, back):
-        k = n_col - 1 + n_ch - 1 + (d - 1) * (n_col - 1) + c - 1
+        k = first_cross + n_ch - 1 + (d - 1) * (n_col - 1) + c - 1
         return spread(c, back, lax.rem(me_ch + n_ch - d, n_ch), k)
 
-    for c in range(1, n_col):
-        spread(c, False, me_ch, c - 1).start()
+    for k in range(HALVES):
+        for d in range(1, n_row):
+            along_row(d, True, k).wait_recv()
+        total = gram_row[0, half(k)]
+        for z in range(1, n_row):
+            total = total + gram_row[z, half(k)]
+        under = jnp.dot(
+            total[:, :rank], cf_ref[...], precision=lax.Precision.HIGHEST,
+            preferred_element_type=jnp.float32,
+        )
+        start = pl.multiple_of(me_col * share + k * lines, lines)
+        own_cf = cf_ref[pl.ds(start, lines), :]
+        nc[me_ch, me_col, half(k)] = own_cf * total[:, rank:] / (under + epsilon)
+        for c in range(1, n_col):
+            spread_half(c, False, k).start()
     for d in range(1, n_ch):
         cross(d, False).start()
-    for c in range(1, n_col):
-        spread(c, True, me_ch, c - 1).wait_recv()
+    for k in range(HALVES):
+        for c in range(1, n_col):
+            spread_half(c, True, k).wait_recv()
 
     mine = nc[me_ch].reshape(rank, chans)
     nc_out[...] = mine
@@ -578,15 +586,16 @@
 
     gathered = gram_row.at[pl.ds(0, n_row - 1)]
     pltpu.make_async_remote_copy(
-        gram_in, gram_in, g_send.at[0], g_recv.at[0],
+        gram_in, gram_in, g_send.at[0], g_recv.at[0, 0],
         device_id={"col": lax.rem(me_col + 1, n_col)}, device_id_type=MESH,
     ).wait_send()
     pltpu.make_async_remote_copy(
-        gathered, gathered, z_send.at[0], z_recv.at[0],
+        gathered, gathered, z_send.at[0], z_recv.at[0, 0],
         device_id={"row": lax.rem(me_row + 1, n_row)}, device_id_type=MESH,
     ).wait_send()
-    for c in range(1, n_col):
-        spread(c, False, me_ch, c - 1).wait_send()
+    for k in range(HALVES):
+        for c in range(1, n_col):
+            spread_half(c, False, k).wait_send()
     for d in range(1, n_ch):
         cross(d, False).wait_send()
         for c in range(1, n_col):
@@ -714,6 +723,7 @@
     share = rank // n_col
     early = rows - EARLY
     pieces = (early - SMOOTH) // CHUNK + 2 * (rank // BAND)
+    news = n_col * n_ch - 1 + (n_col - 1) * (HALVES - 1)
     tall = rows + 2 * SMOOTH
     wide = cols + LANES
     halves, groups = cols // LANES, rows // SUB
@@ -754,9 +764,9 @@
             pltpu.VMEM((tall, rank, wide), f32),
             dma((2, halves, groups)),
             dma((n_ch - 1, halves)), dma((n_ch - 1, halves)),
-            dma((1,)), dma((n_col - 1,)),
-            dma((1,)), dma((n_row - 1,)),
-            dma((n_col * n_ch - 1,)), dma((n_col * n_ch - 1,)),
+            dma((1,)), dma((n_col - 1, HALVES)),
+            dma((1,)), dma((n_row - 1, HALVES)),
+            dma((news,)), dma((news,)),
             dma((n_ch - 1,)), dma((n_ch - 1, pieces)),
             dma((2,)), dma((2, pieces + 1)),
             dma((2,)), dma((2,)),

time: 67.1 us -> 67.4 us (level)
  no operation moved by 1% of the time
where the time goes in v5:
time: 67.4 us; the launch traced here: 66.4 us
  Pallas kernels  65.7 us (97%)
    pallas_call x1, Pallas kernels, shards(): pl.pallas_call(functools.partial(factor_kernel, sizes), out_shape=(pltpu....  64.3 us
    pallas_call x1, Pallas kernels, shards(): pl.pallas_call(store_kernel, out_shape=(jax.ShapeDtypeStruct(pixel_factor...  1.41 us

profile of v5, /device:TPU:1, one launch (start us, length us, event | category | flops | bytes accessed | tf_op | source)
XLA Modules:
  0.0 66.4 jit_solution(14277397789719805853)
XLA Ops:
  0.6 64.3 %factor.1 = (f32[2,4,64,8,128]{4,3,2,1,0:T(8,128)S(1)}, f32[64,192]{1,0:T(8,128)S(1)}) custom-call(f32[192,32,256]{2,1,0:T(8,128)} %x_hbm.1, f32[64,32,256]{2,1,0:T(8,128)} %w_hbm.1, f32[64,192]{1,0:T(8,128)} %cf_hbm.1, s32[32,256]{1,0:T(8,128)} %lab_hbm.1), custom_call_target="tpu_custom_call" | custom-call | tf_op jit(solution)/shard_map/factor/pallas_call | solution.py:734
  65.0 1.4 %store.1 = (f32[64,32,256]{2,1,0:T(8,128)}, f32[64,192]{1,0:T(8,128)}) custom-call(f32[2,4,64,8,128]{4,3,2,1,0:T(8,128)S(1)} %get-tuple-element.4.done, f32[64,192]{1,0:T(8,128)S(1)} %get-tuple-element.5.new_channel), custom_call_target="tpu_custom_call" | custom-call | tf_op jit(solution)/shard_map/store/pallas_call | solution.py:782
